TPU v7x, 256 devices: a whole 4x4x8 slice. The times are simulated.
256 devices in a mesh: occ: 64 (over z, y, x_lo), vir: 4 (over x_hi, core).
Axes of the slice: x: 4 (x_hi: 2, x_lo: 2; x = x_hi * 2 + x_lo), y: 4, z: 8, core: 2. Of those that a mesh axis runs over, the one named last changes fastest.
Arguments:
- factors: bfloat16 [2, 3072, 6144], P(None, 'occ', 'vir'), may hold values from -0.41992188 to 0.41992188
- occ_energy: float32 [2], replicated, may hold values from -1.2 to -0.4
- vir_energy: float32 [3072], replicated, may hold values from 0.4 to 2.5
- block_lengths: int32 [4, 64], replicated, may hold values from 1 to 64, 1536 in all within a row
- block_owner: int32 [4, 64], replicated, may hold values from 0 to 63, each once within a row
Outputs:
- gamma_owned: bfloat16 [16384, 2, 3072], P(('occ', 'vir'))
Inputs may be any that keep to these rules, and one draw needn't show every extreme that they name: `block_lengths`: each row sums to 1536, and every row's largest entry is exactly 64. `block_owner`: each row names every owner index once.
All inputs are finite; a program needn't handle non-finite values.
Results may differ from a plain program's by a relative error of at most 0.0037.
Values may be sent and summed in bfloat16 or wider, within the bound.
A program may use at most 64 MiB of HBM per device.

v0:
```python
import jax
import jax.numpy as jnp
from jax import lax
from jax.sharding import PartitionSpec as P


def pair_terms(own_block, arrived):
    return jnp.einsum("iap,jbp->ijab", own_block, arrived, preferred_element_type=jnp.float32)


def amplitudes(pair_block, occupied_sum, near_energy, far_energy):
    denominator = (
        occupied_sum[:, :, None, None]
        - near_energy[None, None, :, None]
        - far_energy[None, None, None, :]
    )
    swapped = jnp.transpose(pair_block, (1, 0, 2, 3))
    return ((2.0 * pair_block - swapped) / denominator).astype(jnp.bfloat16)


def per_device(factors, occ_energy, vir_energy, block_lengths, block_owner):
    cycle_size = lax.axis_size("occ")
    cycle_index = lax.axis_index("occ")
    quarter_index = lax.axis_index("vir")
    occupied, tile_rows, quarter_width = factors.shape
    occupied_sum = occ_energy[:, None] + occ_energy[None, :]
    near_energy = lax.dynamic_slice_in_dim(vir_energy, cycle_index * tile_rows, tile_rows)
    every_tile = lax.all_gather(factors, "occ", axis=1, tiled=True)
    pair_block = pair_terms(factors, every_tile)
    summed = lax.psum(pair_block.reshape(-1), "vir").reshape(pair_block.shape)
    amplitude = amplitudes(summed, occupied_sum, near_energy, vir_energy)
    accum_gamma = jnp.einsum(
        "ijab,jbp->iap", amplitude, every_tile, preferred_element_type=jnp.float32
    )
    gamma_local = accum_gamma.astype(jnp.bfloat16)
    capacity = 8 * quarter_width // (3 * cycle_size)
    lengths_row = lax.dynamic_index_in_dim(block_lengths, quarter_index, 0, keepdims=False)
    owners_row = lax.dynamic_index_in_dim(block_owner, quarter_index, 0, keepdims=False)
    starts_row = jnp.cumsum(lengths_row) - lengths_row
    owner_match = owners_row[None, :] == jnp.arange(cycle_size, dtype=jnp.int32)[:, None]
    dest_start = jnp.sum(jnp.where(owner_match, starts_row[None, :], 0), axis=1)
    dest_length = jnp.sum(jnp.where(owner_match, lengths_row[None, :], 0), axis=1)
    slot_index = jnp.arange(capacity, dtype=jnp.int32)
    columns = jnp.minimum(dest_start[:, None] + slot_index[None, :], quarter_width - 1)
    live_slot = slot_index[None, :] < dest_length[:, None]
    by_column = jnp.transpose(gamma_local, (2, 0, 1))
    picked = jnp.take(by_column, columns.reshape(-1), axis=0)
    picked = jnp.where(live_slot.reshape(-1)[:, None, None], picked, jnp.zeros((), jnp.bfloat16))
    outgoing = picked.reshape(cycle_size, capacity * occupied * tile_rows)
    incoming = lax.all_to_all(outgoing, "occ", split_axis=0, concat_axis=0, tiled=True)
    incoming = incoming.reshape(cycle_size, capacity, occupied, tile_rows)
    return jnp.transpose(incoming, (1, 2, 0, 3)).reshape(capacity, occupied, cycle_size * tile_rows)


def solution(mesh):
    placed = (P(None, "occ", "vir"), P(), P(), P(), P())
    return jax.shard_map(
        per_device,
        mesh=mesh,
        in_specs=placed,
        out_specs=P(("occ", "vir"), None, None),
        check_vma=False,
    )
```

profile of v0, /device:TPU:1, one launch (start us, length us, event | category | flops | bytes accessed | tf_op | source)
XLA Modules:
  0.0 637.0 jit_solution(3104799769309652020)
XLA Ops:
  6.5 0.0 all-gather.2.cloned.1.call-start
  6.5 0.7 all-gather.2.cloned.1.call-update
  7.3 0.0 all-reduce.2.cloned.1.call-start
  7.3 0.7 constant_dynamic-slice_fusion
  8.0 0.2 reduce-window_clone.1
  8.2 0.7 subtract_bitcast_fusion
  8.9 417.6 %all-gather.2.cloned.1.call-done = bf16[2,3072,1536]{2,1,0:T(8,128)(2,1)} async-done(((bf16[2,48,1536]{2,1,0:T(8,128)(2,1)}), bf16[2,3072,1536]{2,1,0:T(8,128)(2,1)}) %all-gather.2.cloned.1.call-update) | async-done | bytes 18874384 | tf_op jit(solution)/shard_map/all_gather | solution.py:28
  426.5 13.6 %fusion.4 = f32[2,2,48,3072]{3,2,0,1:T(8,128)} fusion(bf16[2,3072,1536]{2,1,0:T(8,128)(2,1)} %all-gather.2.cloned.1.call-done, bf16[2,48,1536]{2,1,0:T(8,128)(2,1)} %param.5), kind=kOutput, calls=%fused_computation.7 | convolution fusion | flops 1811939328 | bytes 21528576 | tf_op jit(solution)/shard_map/iap,jbp->ijab/dot_general | solution.py:8
  440.1 0.0 copy-start.1
  440.1 0.0 copy-start
  440.1 0.0 all-reduce.2.cloned.1.call-update
  440.2 0.7 fusion.24
  440.8 0.1 select_reduce_fusion
  441.0 0.1 add_minimum_fusion
  441.0 0.1 min.28
  441.1 0.1 min.26
  441.2 0.1 iota_compare_fusion.1
  441.3 0.1 lt.55
  441.4 0.0 copy-done.1
  441.4 0.1 dynamic_slice.12
  441.5 0.0 copy-done
  441.5 0.1 broadcast_add_fusion
  441.5 0.1 broadcast_subtract_fusion
  441.7 69.3 %all-reduce.2.cloned.1.call-done = f32[2,2,48,3072]{3,2,0,1:T(8,128)} async-done(((f32[2,2,48,3072]{3,2,0,1:T(8,128)}), f32[2,2,48,3072]{3,2,0,1:T(8,128)}) %all-reduce.2.cloned.1.call-update) | async-done | bytes 2359312 | tf_op jit(solution)/shard_map/psum | solution.py:30
  511.0 11.0 %fusion.15 = bf16[1536,2,48]{0,2,1:T(8,128)(2,1)S(1)} fusion(bf16[2,3072,1536]{2,1,0:T(8,128)(2,1)} %all-gather.2.cloned.1.call-done, f32[2,2,48,3072]{3,2,0,1:T(8,128)} %all-reduce.2.cloned.1.call-done, f32[3072]{0:T(1024)S(1)} %copy-done.1, f32[2,2,48]{2,1,0:T(2,128)S(1)} %broadcast_subtract_fusion), kind=kOutput, calls=%fused_computation.14 | convolution fusion | flops 1815035904 | bytes 21541632 | tf_op jit(solution)/shard_map/ijab,jbp->iap/dot_general | solution.py:32
  522.0 0.6 copy.17
  522.6 26.9 %gather_fusion = bf16[4096,2,48]{2,1,0:T(2,128)(2,1)} fusion(bf16[1536,2,48]{2,1,0:T(2,128)(2,1)S(1)} %copy.17, s32[4096]{0:T(1024)S(1)} %broadcast_clamp_fusion), kind=kCustom, calls=%fused_computation | custom fusion | bytes 1589248 | tf_op jit(solution)/shard_map/jit(_take)/gather | solution.py:47
  549.5 19.9 %broadcast_select_fusion.1 = bf16[4096,2,48]{2,1,0:T(2,128)(2,1)S(1)} fusion(pred[4096]{0:T(1024)(128)(4,1)S(1)} %lt.55, bf16[4096,2,48]{2,1,0:T(2,128)(2,1)} %gather_fusion, pred[4096]{0:T(1024)(128)(4,1)S(1)} %compare_and_fusion), kind=kLoop, calls=%fused_computation.6 | loop fusion | flops 786432 | bytes 1581056 | tf_op jit(solution)/shard_map/jit(_where)/select_n | solution.py:48
  569.4 4.4 select_n.68
  573.8 0.5 broadcast.106
  574.4 6.4 %reduce.1 = bf16[64,6144]{1,0:T(8,128)(2,1)S(1)} reduce(bf16[64,1,6144]{2,1,0:T(2,128)(2,1)} %select_n.68, bf16[]{:T(256)} %broadcast.106), dimensions={1}, to_apply=%select_n.68.reduce_sub_computation | reduce | bytes 1572866 | tf_op jit(solution)/shard_map/jit(_where)/select_n | solution.py:48
  580.8 0.6 reshape.171
  581.3 31.5 %all_to_all.6 = bf16[64,2,3072]{2,1,0:T(2,128)(2,1)S(1)} all-to-all(bf16[64,2,3072]{2,1,0:T(2,128)(2,1)S(1)} %reshape.171), channel_id=1, replica_groups=mesh['occ'=64,'vir'=4] {'occ'}, dimensions={0} | all-to-all | bytes 1572864 | tf_op jit(solution)/shard_map/all_to_all | solution.py:50
  612.9 0.6 reshape.172
  613.5 4.7 reduce
  618.2 2.2 reshape.155
  620.4 3.8 copy.23
  624.2 5.9 reshape.169
  (3 shorter events, 0.0 us)
Async XLA Ops:
  6.5 420.0 %all-gather.2.cloned.1.call-start = ((), (), s32[]{:S(2)}) async-start(), calls=%async_computation.1 | async-start | bytes 19169280 | tf_op jit(solution)/shard_map/all_gather | solution.py:28
  7.3 503.8 %all-reduce.2.cloned.1.call-start = ((), (), s32[]{:S(2)}) async-start(), calls=%async_computation.2 | async-start | bytes 4718592 | tf_op jit(solution)/shard_map/psum | solution.py:30
  440.1 1.3 copy-start.1
  440.1 1.3 copy-start
Sparse Core Ops, SparseCore 0:
  9.1 417.3 all-gather.1
  440.3 70.6 all-reduce.1
where the time goes:
time: 638 us; the launch traced here: 637 us
  waiting for transfers between devices  488 us (76%)
  local copies, waits for them, and re-layouts  47.3 us (7%)
  other arithmetic  32.4 us (5%)
  blocking collectives  31.5 us (5%)
  matrix products  24.6 us (4%)
  between operations  13.5 us (2%)
    all_gather x1, waiting for transfers between devices, per_device(): every_tile = lax.all_gather(factors, 'occ', axis=1, tiled=True)  418 us
    psum x1, waiting for transfers between devices, per_device(): summed = lax.psum(pair_block.reshape(-1), 'vir').reshape(pair_block.shape)  69.3 us
    all_to_all x1, blocking collectives, per_device(): lax.all_to_all(outgoing, 'occ', split_axis=0, concat_axis=0, tiled=True)  31.5 us
    gather x1, local copies, waits for them, and re-layouts, per_device(): picked = jnp.take(by_column, columns.reshape(-1), axis=0)  26.9 us
    select_n x2, other arithmetic, per_device(): jnp.where(live_slot.reshape(-1)[:, None, None], picked, jnp.zeros((), jnp...  26.3 us
    dot_general x1, matrix products, pair_terms(): jnp.einsum('iap,jbp->ijab', own_block, arrived, preferred_element_type=jn...  13.6 us
  transfers between devices with their start and end apart: 2, of which 2 were waited for; matrix products, arithmetic and copies ran while one was open for 0% of the time, Pallas kernels for 0%

commit v1 on v0

v1 whole, which is shorter than its diff:
```python
import jax
import jax.numpy as jnp
from jax import lax
from jax.sharding import Mesh, PartitionSpec as P

ROW = ("y", "xl")
VIR = ("xh", "core")


def per_device(factors, occ_energy, vir_energy, block_lengths, block_owner):
    zi = lax.axis_index("z")
    yx = lax.axis_index(ROW)
    nz = lax.axis_size("z")
    nyx = lax.axis_size(ROW)
    cycle_size = nz * nyx
    quarter_index = lax.axis_index(VIR)
    occupied, tile_rows, width = factors.shape
    group = tile_rows * nyx
    row_block = lax.all_gather(factors, ROW, axis=1, tiled=True)
    col_block = lax.all_gather(factors, "z", axis=1, tiled=True)
    pair = jnp.einsum("iap,jbp->ijab", row_block, col_block, preferred_element_type=jnp.float32)
    pair = lax.psum(pair.reshape(-1), VIR).reshape(pair.shape)
    occupied_sum = occ_energy[:, None] + occ_energy[None, :]
    row_energy = lax.dynamic_slice_in_dim(vir_energy, zi * group, group)
    col_energy = lax.dynamic_index_in_dim(
        vir_energy.reshape(nz, nyx, tile_rows), yx, 1, keepdims=False
    ).reshape(-1)
    denominator = (
        occupied_sum[:, :, None, None] - row_energy[None, None, :, None] - col_energy[None, None, None, :]
    )
    amplitude = ((2.0 * pair - jnp.transpose(pair, (1, 0, 2, 3))) / denominator).astype(jnp.bfloat16)
    partial = jnp.einsum("ijab,jbp->iap", amplitude, col_block, preferred_element_type=jnp.float32)
    gamma = lax.psum_scatter(partial, ROW, scatter_dimension=1, tiled=True).astype(jnp.bfloat16)
    capacity = 8 * width // (3 * cycle_size)
    lengths_row = lax.dynamic_index_in_dim(block_lengths, quarter_index, 0, keepdims=False)
    owners_row = lax.dynamic_index_in_dim(block_owner, quarter_index, 0, keepdims=False)
    starts_row = jnp.cumsum(lengths_row) - lengths_row
    owner_match = owners_row[None, :] == jnp.arange(cycle_size, dtype=jnp.int32)[:, None]
    dest_start = jnp.sum(jnp.where(owner_match, starts_row[None, :], 0), axis=1)
    dest_length = jnp.sum(jnp.where(owner_match, lengths_row[None, :], 0), axis=1)
    slot_index = jnp.arange(capacity, dtype=jnp.int32)
    columns = jnp.where(
        slot_index[None, :] < dest_length[:, None], dest_start[:, None] + slot_index[None, :], -1
    ).reshape(-1)
    chosen = (columns[:, None] == jnp.arange(width, dtype=jnp.int32)[None, :]).astype(jnp.bfloat16)
    picked = jnp.einsum("sp,iap->sia", chosen, gamma, preferred_element_type=jnp.float32)
    picked = picked.astype(jnp.bfloat16)
    outgoing = picked.reshape(cycle_size, capacity * occupied * tile_rows)
    incoming = lax.all_to_all(outgoing, ("z",) + ROW, split_axis=0, concat_axis=0, tiled=True)
    incoming = incoming.reshape(cycle_size, capacity, occupied, tile_rows)
    return jnp.transpose(incoming, (1, 2, 0, 3)).reshape(capacity, occupied, cycle_size * tile_rows)


def solution(mesh):
    fine = Mesh(mesh.devices.reshape(8, 4, 2, 2, 2), ("z", "y", "xl", "xh", "core"))
    placed = (P(None, ("z", "y", "xl"), VIR), P(), P(), P(), P())
    return jax.shard_map(
        per_device,
        mesh=fine,
        in_specs=placed,
        out_specs=P(("z", "y", "xl", "xh", "core"), None, None),
        check_vma=False,
    )
```

time: 638 us -> 375 us (0.59)
  waiting for transfers between devices: 488 us -> 275 us
  local copies, waits for them, and re-layouts: 47.3 us -> 22.4 us
  other arithmetic: 32.4 us -> 12.4 us
    all_gather x1 -> x2, waiting for transfers between devices: 418 us -> 106 us  [the longest x1 63.3 us: per_device(): row_block = lax.all_gather(factors, ROW, axis=1, tiled=True)]
    reduce_scatter x0 -> x1, waiting for transfers between devices: none -> 100 us  [per_device(): lax.psum_scatter(partial, ROW, scatter_dimension=1, tiled=True)]
    gather x1 -> x0, local copies, waits for them, and re-layouts: 26.9 us -> none  [per_device(): picked = jnp.take(by_column, columns.reshape(-1), axis=0)]
    select_n x3 -> x1, other arithmetic: 26.3 us -> 0.09 us  [per_device(): jnp.where(slot_index[None, :] < dest_length[:, None], dest_start[:, None]...]
    all_to_all x1 -> x2, other arithmetic: 4.71 us -> 11.1 us  [per_device(): lax.all_to_all(outgoing, ('z',) + ROW, split_axis=0, concat_axis=0, tiled...]
    dot_general x2 -> x3, matrix products: 24.6 us -> 19.4 us  [the longest x1 6.97 us: per_device(): jnp.einsum('sp,iap->sia', chosen, gamma, preferred_element_type=jnp.float32)]
  transfers between devices with their start and end apart: 2 -> 4, of which waited for: 2 -> 4; matrix products, arithmetic and copies ran while one was open for 0% -> 0% of each run, Pallas kernels for 0% -> 0%
where the time goes in v1:
time: 375 us; the launch traced here: 374 us
  waiting for transfers between devices  275 us (73%)
  blocking collectives  31.2 us (8%)
  local copies, waits for them, and re-layouts  22.4 us (6%)
  matrix products  19.4 us (5%)
  between operations  13.2 us (4%)
  other arithmetic  12.4 us (3%)
    reduce_scatter x1, waiting for transfers between devices, per_device(): lax.psum_scatter(partial, ROW, scatter_dimension=1, tiled=True)  100 us
    psum x1, waiting for transfers between devices, per_device(): pair = lax.psum(pair.reshape(-1), VIR).reshape(pair.shape)  67.3 us
    all_gather x1, waiting for transfers between devices, per_device(): row_block = lax.all_gather(factors, ROW, axis=1, tiled=True)  63.3 us
    all_gather x1, waiting for transfers between devices, per_device(): col_block = lax.all_gather(factors, 'z', axis=1, tiled=True)  42.4 us
    all_to_all x1, blocking collectives, per_device(): lax.all_to_all(outgoing, ('z',) + ROW, split_axis=0, concat_axis=0, tiled...  31.2 us
    all_to_all x2, other arithmetic, per_device(): lax.all_to_all(outgoing, ('z',) + ROW, split_axis=0, concat_axis=0, tiled...  11.1 us
    reshape x2, local copies, waits for them, and re-layouts, per_device(): jnp.transpose(incoming, (1, 2, 0, 3))  9.72 us
  transfers between devices with their start and end apart: 4, of which 4 were waited for; matrix products, arithmetic and copies ran while one was open for 0% of the time, Pallas kernels for 0%

profile of v1, /device:TPU:1, one launch (start us, length us, event | category | flops | bytes accessed | tf_op | source)
XLA Modules:
  0.0 373.7 jit_solution(16632524327149536762)
XLA Ops:
  6.5 0.0 all-gather.3.cloned.1.call-start
  6.5 0.7 all-gather.3.cloned.1.call-update
  7.3 0.0 all-gather.5.cloned.1.call-start
  7.3 0.7 all-gather.5.cloned.1.call-update
  8.0 0.0 all-reduce.2.cloned.1.call-start
  8.1 42.4 %all-gather.3.cloned.1.call-done = bf16[2,384,1536]{2,1,0:T(8,128)(2,1)} async-done(((bf16[2,48,1536]{2,1,0:T(8,128)(2,1)}), bf16[2,384,1536]{2,1,0:T(8,128)(2,1)}) %all-gather.3.cloned.1.call-update) | async-done | bytes 2359312 | tf_op jit(solution)/shard_map/all_gather | solution.py:20
  50.5 63.3 %all-gather.5.cloned.1.call-done = bf16[2,384,1536]{2,1,0:T(8,128)(2,1)} async-done(((bf16[2,48,1536]{2,1,0:T(8,128)(2,1)}), bf16[2,384,1536]{2,1,0:T(8,128)(2,1)}) %all-gather.5.cloned.1.call-update) | async-done | bytes 2359312 | tf_op jit(solution)/shard_map/all_gather | solution.py:19
  113.8 5.8 %fusion.13 = f32[2,2,384,384]{2,3,0,1:T(8,128)} fusion(bf16[2,384,1536]{2,1,0:T(8,128)(2,1)} %all-gather.5.cloned.1.call-done, bf16[2,384,1536]{2,1,0:T(8,128)(2,1)} %all-gather.3.cloned.1.call-done), kind=kOutput, calls=%fused_computation.14 | convolution fusion | flops 1811939328 | bytes 7077888 | tf_op jit(solution)/shard_map/iap,jbp->ijab/dot_general | solution.py:21
  119.6 0.0 copy-start
  119.6 0.0 copy-start.1
  119.6 0.0 copy-start.3
  119.6 0.0 all-reduce.2.cloned.1.call-update
  119.6 0.0 reduce-scatter.2.cloned.1.call-start
  119.7 0.6 copy-done
  120.3 0.1 reshape.97
  120.4 0.1 sub.46
  120.5 0.1 dynamic_slice.16
  120.5 0.0 copy-done.1
  120.5 0.1 broadcast_add_fusion
  120.6 0.1 broadcast_subtract_fusion
  120.7 67.3 %all-reduce.2.cloned.1.call-done = f32[2,2,384,384]{2,3,0,1:T(8,128)} async-done(((f32[2,2,384,384]{2,3,0,1:T(8,128)}), f32[2,2,384,384]{2,3,0,1:T(8,128)}) %all-reduce.2.cloned.1.call-update) | async-done | bytes 2359312 | tf_op jit(solution)/shard_map/psum | solution.py:22
  188.0 0.0 copy-done.3
  188.0 6.6 %convolution_bitcast_fusion = f32[2,384,1536]{2,1,0:T(8,128)} fusion(bf16[2,384,1536]{2,1,0:T(8,128)(2,1)S(1)} %copy-done.3, f32[2,2,384,384]{2,3,0,1:T(8,128)} %all-reduce.2.cloned.1.call-done, f32[384]{0:T(512)S(1)} %sub.46, f32[2,2,384]{2,1,0:T(2,128)S(1)} %broadcast_subtract_fusion), kind=kOutput, calls=%fused_computation.5 | convolution fusion | flops 1814888448 | bytes 9444864 | tf_op jit(solution)/shard_map/ijab,jbp->iap/dot_general | solution.py:32
  194.6 0.0 copy-start.2
  194.6 0.0 reduce-scatter.2.cloned.1.call-update
  194.7 0.6 copy-done.2
  195.3 0.2 reduce-window_clone.1
  195.6 0.7 fusion.23
  196.3 0.1 select_reduce_fusion.1
  196.4 0.1 add_select_fusion
  196.5 0.1 select_n.34
  196.5 100.5 %reduce-scatter.2.cloned.1.call-done = f32[2,48,1536]{2,1,0:T(8,128)} async-done(((f32[2,384,1536]{2,1,0:T(8,128)}), f32[2,48,1536]{2,1,0:T(8,128)}) %reduce-scatter.2.cloned.1.call-update) | async-done | bytes 589840 | tf_op jit(solution)/shard_map/reduce_scatter | solution.py:33
  297.0 7.0 %fusion.4 = bf16[4096,2,48]{0,2,1:T(8,128)(2,1)S(1)} fusion(s32[4096]{0:T(1024)S(1)} %select_n.34, f32[2,48,1536]{2,1,0:T(8,128)} %reduce-scatter.2.cloned.1.call-done), kind=kOutput, calls=%fused_computation.4 | convolution fusion | flops 1214791680 | bytes 1392640 | tf_op jit(solution)/shard_map/sp,iap->sia/dot_general | solution.py:46
  304.0 2.8 copy.19
  306.8 4.4 %all_to_all.8 = bf16[64,1,6144]{2,1,0:T(2,128)(2,1)} reshape(bf16[4096,2,48]{2,1,0:T(2,128)(2,1)S(1)} %copy.19) | data formatting | bytes 1572864 | tf_op jit(solution)/shard_map/all_to_all | solution.py:49
  311.2 0.5 broadcast.52
  311.7 6.4 %reduce.5 = bf16[64,6144]{1,0:T(8,128)(2,1)S(1)} reduce(bf16[64,1,6144]{2,1,0:T(2,128)(2,1)} %all_to_all.8, bf16[]{:T(256)} %broadcast.52), dimensions={1}, to_apply=%all_to_all.8.reduce_sub_computation | reduce | bytes 1572866 | tf_op jit(solution)/shard_map/all_to_all | solution.py:49
  318.1 0.6 reshape.114
  318.7 31.2 %all_to_all.10 = bf16[64,2,3072]{2,1,0:T(2,128)(2,1)S(1)} all-to-all(bf16[64,2,3072]{2,1,0:T(2,128)(2,1)S(1)} %reshape.114), channel_id=1, replica_groups=mesh['z'=8,'y'=4,'xl'=2,'xh'=2,'core'=2] {'z','y','xl'}, dimensions={0} | all-to-all | bytes 1572864 | tf_op jit(solution)/shard_map/all_to_all | solution.py:49
  349.9 0.6 reshape.115
  350.6 4.7 %reduce.1 = bf16[64,6144]{1,0:T(8,128)(2,1)S(1)} reduce(bf16[64,1,6144]{2,1,0:T(2,128)(2,1)S(1)} %reshape.115, bf16[]{:T(256)} %constant.48), dimensions={1}, to_apply=%all_to_all.7.reduce_sub_computation | reduce | bytes 1572866 | tf_op jit(solution)/shard_map/all_to_all | solution.py:49
  355.3 2.2 reshape.98
  357.5 3.8 %copy.26 = bf16[64,2,64,48]{3,2,1,0:T(8,128)(2,1)} copy(bf16[64,2,64,48]{3,1,0,2:T(2,128)(2,1)S(1)} %bitcast.40) | data formatting | bytes 1572864 | tf_op jit(solution)/shard_map/reshape | solution.py:51
  361.3 5.9 %reshape.105 = bf16[64,2,3072]{2,1,0:T(2,128)(2,1)} reshape(bf16[64,2,64,48]{3,2,1,0:T(8,128)(2,1)} %copy.26) | data formatting | bytes 1572864 | tf_op jit(solution)/shard_map/reshape | solution.py:51
  (3 shorter events, 0.0 us)
Async XLA Ops:
  6.5 44.0 %all-gather.3.cloned.1.call-start = ((), (), s32[]{:S(2)}) async-start(), calls=%async_computation.2 | async-start | bytes 2654208 | tf_op jit(solution)/shard_map/all_gather | solution.py:20
  7.3 106.5 %all-gather.5.cloned.1.call-start = ((), (), s32[]{:S(2)}) async-start(), calls=%async_computation.3 | async-start | bytes 2654208 | tf_op jit(solution)/shard_map/all_gather | solution.py:19
  8.0 180.0 %all-reduce.2.cloned.1.call-start = ((), (), s32[]{:S(2)}) async-start(), calls=%async_computation.4 | async-start | bytes 4718592 | tf_op jit(solution)/shard_map/psum | solution.py:22
  119.6 0.7 copy-start
  119.6 1.0 copy-start.1
  119.6 68.4 %copy-start.3 = (bf16[2,384,1536]{2,1,0:T(8,128)(2,1)S(1)}, bf16[2,384,1536]{2,1,0:T(8,128)(2,1)}, u32[]{:S(2)}) copy-start(bf16[2,384,1536]{2,1,0:T(8,128)(2,1)} %all-gather.3.cloned.1.call-done) | copy-start | bytes 7077892
  119.6 177.4 %reduce-scatter.2.cloned.1.call-start = ((), (), s32[]{:S(2)}) async-start(), calls=%async_computation.5 | async-start | bytes 5308416 | tf_op jit(solution)/shard_map/reduce_scatter | solution.py:33
  194.6 0.7 copy-start.2
Sparse Core Ops, SparseCore 0:
  9.1 41.3 all-gather.2
  52.3 61.4 all-gather.4
  119.7 68.2 all-reduce.1
  194.8 102.1 reduce-scatter.1

commit v2 on v1

v2 whole, which is shorter than its diff:
```python
import jax
import jax.numpy as jnp
from jax import lax
from jax.experimental import pallas as pl
from jax.experimental.pallas import tpu as pltpu
from jax.sharding import Mesh, PartitionSpec as P

ROW = ("y", "xl")
VIR = ("xh", "core")
F32 = jnp.float32
BF16 = jnp.bfloat16


def ring(axis, shift):
    n = lax.axis_size(axis)
    return lax.rem(lax.axis_index(axis) + shift + n, n)


def flip(axis):
    return 1 - lax.axis_index(axis)


def gamma_kernel(
    f_ref, occ_ref, row_e_ref, col_e_ref, out_ref,
    rbuf, cbuf, m_send, m_own, m_recv, h_send, h_recv, abuf, part,
    a_send, a_recv, b_send, b_recv, x_out, x_recv,
    zs, zr, ys, yr, xs, xr, ms, mr, hs, hr, as_, ar, pas, par, pbs, pbr, pxs, pxr,
):
    z, y, xl, xh, core = (lax.axis_index(n) for n in ("z", "y", "xl", "xh", "core"))
    rows = f_ref.shape[1]
    width = f_ref.shape[2]

    barrier = pltpu.get_barrier_semaphore()
    peers = [
        {"z": ring("z", 1)}, {"z": ring("z", -1)}, {"y": ring("y", 1)}, {"y": ring("y", -1)},
        {"xl": flip("xl")}, {"xh": flip("xh")}, {"core": flip("core")},
    ]
    for peer in peers:
        pl.semaphore_signal(barrier, inc=1, device_id=peer, device_id_type=pl.DeviceIdType.MESH)
    pl.semaphore_wait(barrier, len(peers))

    started = []

    def send(src, dst, ssem, rsem, peer):
        copy = pltpu.make_async_remote_copy(
            src_ref=src, dst_ref=dst, send_sem=ssem, recv_sem=rsem,
            device_id=peer, device_id_type=pl.DeviceIdType.MESH,
        )
        copy.start()
        started.append(copy)
        return copy

    def arrive(dst, rsem):
        pltpu.make_async_remote_copy(
            src_ref=dst, dst_ref=dst, send_sem=rsem, recv_sem=rsem,
            device_id=peers[0], device_id_type=pl.DeviceIdType.MESH,
        ).wait_recv()

    def yx(dy, other):
        return ring("y", dy) * 2 + (flip("xl") if other else xl)

    z_to = ({"z": ring("z", 1)}, {"z": ring("z", -1)})
    y_to = ({"y": ring("y", 1)}, {"y": ring("y", -1)})
    x_to = {"xl": flip("xl")}

    def z_send(d, step, i):
        origin = ring("z", (1 - step) if d == 0 else (step - 1))
        src = f_ref.at[i] if step == 1 else cbuf.at[i, origin]
        send(src, cbuf.at[i, origin], zs.at[d, step - 1, i], zr.at[d, step - 1, i], z_to[d])

    def z_arrive(d, step, i):
        origin = ring("z", -step if d == 0 else step)
        arrive(cbuf.at[i, origin], zr.at[d, step - 1, i])

    def y_send(d, k, i, dy, other):
        src = f_ref.at[i] if (dy == 0 and not other) else rbuf.at[i, yx(dy, other)]
        send(src, rbuf.at[i, yx(dy, other)], ys.at[d, k], yr.at[d, k], y_to[d])

    def y_arrive(d, k, i, dy, other):
        arrive(rbuf.at[i, yx(dy, other)], yr.at[d, k])

    def x_send(k, i, dy):
        src = f_ref.at[i] if dy == 0 else rbuf.at[i, yx(dy, False)]
        send(src, rbuf.at[i, yx(dy, False)], xs.at[k], xr.at[k], x_to)

    def x_arrive(k, i, dy):
        arrive(rbuf.at[i, yx(dy, True)], xr.at[k])

    for i in (0, 1):
        for d in (0, 1):
            z_send(d, 1, i)
            y_send(d, i, i, 0, False)
        x_send(i, i, 0)
    for i in (0, 1):
        cbuf[i, z] = f_ref[i]
        rbuf[i, yx(0, False)] = f_ref[i]
    for d in (0, 1):
        z_arrive(d, 1, 0)
        z_send(d, 2, 0)
    y_arrive(0, 0, 0, -1, False)
    x_send(2, 0, -1)
    y_send(0, 2, 0, -1, False)
    y_arrive(1, 0, 0, 1, False)
    for d in (0, 1):
        z_arrive(d, 1, 1)
        z_send(d, 2, 1)
    y_arrive(1, 1, 1, 1, False)
    x_send(3, 1, 1)
    y_send(1, 2, 1, 1, False)
    x_send(4, 0, 1)
    y_arrive(0, 1, 1, -1, False)
    x_send(5, 1, -1)
    for d in (0, 1):
        z_arrive(d, 2, 0)
        z_send(d, 3, 0)
    x_arrive(0, 0, 0)
    x_arrive(1, 1, 0)
    x_arrive(2, 0, -1)
    y_send(0, 3, 0, -1, True)
    for d in (0, 1):
        z_arrive(d, 2, 1)
        z_send(d, 3, 1)
    x_arrive(3, 1, 1)
    y_send(1, 3, 1, 1, True)
    z_arrive(0, 3, 0)
    z_send(0, 4, 0)
    z_arrive(1, 3, 1)
    z_send(1, 4, 1)
    z_arrive(1, 3, 0)
    z_arrive(0, 3, 1)
    y_arrive(0, 2, 0, -2, False)
    y_arrive(1, 2, 1, 2, False)
    x_arrive(4, 0, 1)
    x_arrive(5, 1, -1)
    y_arrive(0, 3, 0, -2, True)
    y_arrive(1, 3, 1, 2, True)
    z_arrive(0, 4, 0)
    z_arrive(1, 4, 1)

    half = 4 * rows
    side = 8 * rows
    columns = cbuf[...].reshape(2 * side, width)

    def pair_rows(i, h):
        lhs = rbuf[i, pl.ds(h * 4, 4)].reshape(half, width)
        return lax.dot_general(lhs, columns, (((1,), (1,)), ((), ())), preferred_element_type=F32)

    core_to = {"core": flip("core")}
    for i in (0, 1):
        m_send[i] = pair_rows(i, 1 - core)
        send(m_send.at[i], m_recv.at[i], ms.at[i], mr.at[i], core_to)
    for i in (0, 1):
        m_own[i] = pair_rows(i, core)
    xh_to = {"xh": flip("xh")}
    for i in (0, 1):
        arrive(m_recv.at[i], mr.at[i])
        total = m_own[i] + m_recv[i]
        m_own[i] = total
        h_send[i] = total.astype(BF16)
        send(h_send.at[i], h_recv.at[i], hs.at[i], hr.at[i], xh_to)
    for i in (0, 1):
        arrive(h_recv.at[i], hr.at[i])
        m_own[i] = m_own[i] + h_recv[i].astype(F32)
    row_e = row_e_ref[pl.ds(pl.multiple_of(core * half, 16), half), :]
    col_e = col_e_ref[...]
    mine = pl.ds(pl.multiple_of(core * half, 16), half)
    for i in (0, 1):
        for j in (0, 1):
            denominator = (occ_ref[i] + occ_ref[j]) - row_e - col_e
            direct = m_own[i, :, pl.ds(j * side, side)]
            swapped = m_own[j, :, pl.ds(i * side, side)]
            abuf[i, mine, pl.ds(j * side, side)] = ((2.0 * direct - swapped) / denominator).astype(BF16)
        send(abuf.at[i, mine], abuf.at[i, mine], as_.at[i], ar.at[i], core_to)
    theirs = pl.ds(pl.multiple_of((1 - core) * half, 16), half)
    for i in (0, 1):
        arrive(abuf.at[i, theirs], ar.at[i])

    pair_rows2 = 2 * rows

    def partial(slot, dy):
        at = pl.ds(pl.multiple_of(ring("y", dy) * pair_rows2, 16), pair_rows2)
        lhs = abuf[:, at, :].reshape(2 * pair_rows2, 2 * side)
        res = jnp.dot(lhs, cbuf[...].reshape(2 * side, width), preferred_element_type=F32)
        part[slot] = res.reshape(2, pair_rows2, width)

    partial(0, 2)
    for d in (0, 1):
        a_send[d] = part[0, d].astype(BF16)
        send(a_send.at[d], a_recv.at[d], pas.at[d], par.at[d], y_to[d])
    for d in (0, 1):
        partial(1 + d, 1 if d == 0 else -1)
        i = 1 - d
        b_send[d, i] = part[1 + d, i].astype(BF16)
        send(b_send.at[d, i], b_recv.at[d, i], pbs.at[d, i], pbr.at[d, i], y_to[d])
    for d in (0, 1):
        arrive(a_recv.at[d], par.at[d])
        b_send[d, d] = (part[1 + d, d] + a_recv[d].astype(F32)).astype(BF16)
        send(b_send.at[d, d], b_recv.at[d, d], pbs.at[d, d], pbr.at[d, d], y_to[d])
    partial(0, 0)
    own_rows = pl.ds(pl.multiple_of(xl * rows, 16), rows)
    far_rows = pl.ds(pl.multiple_of((1 - xl) * rows, 16), rows)
    for i in (0, 1):
        for d in (0, 1):
            arrive(b_recv.at[d, i], pbr.at[d, i])
        far = part[0, i, far_rows] + b_recv[0, i, far_rows].astype(F32) + b_recv[1, i, far_rows].astype(F32)
        x_out[i] = far.astype(BF16)
        send(x_out.at[i], x_recv.at[i], pxs.at[i], pxr.at[i], x_to)
    for i in (0, 1):
        near = part[0, i, own_rows] + b_recv[0, i, own_rows].astype(F32) + b_recv[1, i, own_rows].astype(F32)
        arrive(x_recv.at[i], pxr.at[i])
        out_ref[i] = (near + x_recv[i].astype(F32)).astype(BF16)
    for copy in started:
        copy.wait_send()


def own_gamma(factors, occ_energy, vir_energy):
    occupied, rows, width = factors.shape
    nz, nyx = lax.axis_size("z"), lax.axis_size(ROW)
    group = rows * nyx
    row_e = lax.dynamic_slice_in_dim(vir_energy, lax.axis_index("z") * group, group).reshape(group, 1)
    col_e = lax.dynamic_index_in_dim(
        vir_energy.reshape(nz, nyx, rows), lax.axis_index(ROW), 1, keepdims=False
    ).reshape(1, group)
    half = group // 2
    dma = pltpu.SemaphoreType.DMA
    vmem = pl.BlockSpec(memory_space=pltpu.VMEM)
    smem = pl.BlockSpec(memory_space=pltpu.SMEM)
    sems = [(2, 4, 2)] * 2 + [(2, 4)] * 2 + [(6,)] * 2 + [(2,)] * 8 + [(2, 2)] * 2 + [(2,)] * 2
    return pl.pallas_call(
        gamma_kernel,
        out_shape=jax.ShapeDtypeStruct((occupied, rows, width), BF16),
        in_specs=[vmem, smem, vmem, vmem],
        out_specs=vmem,
        scratch_shapes=[
            pltpu.VMEM((2, nyx, rows, width), BF16),
            pltpu.VMEM((2, nz, rows, width), BF16),
            pltpu.VMEM((2, half, 2 * group), F32),
            pltpu.VMEM((2, half, 2 * group), F32),
            pltpu.VMEM((2, half, 2 * group), F32),
            pltpu.VMEM((2, half, 2 * group), BF16),
            pltpu.VMEM((2, half, 2 * group), BF16),
            pltpu.VMEM((2, group, 2 * group), BF16),
            pltpu.VMEM((3, 2, 2 * rows, width), F32),
            pltpu.VMEM((2, 2 * rows, width), BF16),
            pltpu.VMEM((2, 2 * rows, width), BF16),
            pltpu.VMEM((2, 2, 2 * rows, width), BF16),
            pltpu.VMEM((2, 2, 2 * rows, width), BF16),
            pltpu.VMEM((2, rows, width), BF16),
            pltpu.VMEM((2, rows, width), BF16),
        ] + [dma(s) for s in sems],
        compiler_params=pltpu.CompilerParams(
            collective_id=0, has_side_effects=True, vmem_limit_bytes=56 * 1024 * 1024
        ),
        name="own_gamma",
    )(factors, occ_energy, row_e, col_e)


def per_device(factors, occ_energy, vir_energy, block_lengths, block_owner):
    occupied, rows, width = factors.shape
    owners = lax.axis_size("z") * lax.axis_size(ROW)
    capacity = 8 * width // (3 * owners)
    quarter = lax.axis_index(VIR)
    lengths = lax.dynamic_index_in_dim(block_lengths, quarter, 0, keepdims=False)
    owner_of = lax.dynamic_index_in_dim(block_owner, quarter, 0, keepdims=False)
    order = jnp.arange(owners, dtype=jnp.int32)
    starts = jnp.sum(jnp.where(order[None, :] < order[:, None], lengths[None, :], 0), axis=1)
    match = owner_of[None, :] == order[:, None]
    dest_start = jnp.sum(jnp.where(match, starts[None, :], 0), axis=1)
    dest_length = jnp.sum(jnp.where(match, lengths[None, :], 0), axis=1)
    slot = jnp.arange(capacity, dtype=jnp.int32)
    columns = jnp.where(slot[None, :] < dest_length[:, None], dest_start[:, None] + slot[None, :], -1)
    gamma = own_gamma(factors, occ_energy, vir_energy)
    chosen = (columns.reshape(-1)[:, None] == jnp.arange(width, dtype=jnp.int32)[None, :]).astype(BF16)
    picked = jnp.einsum("sp,iap->sia", chosen, gamma, preferred_element_type=F32).astype(BF16)
    outgoing = picked.reshape(owners, capacity * occupied * rows)
    incoming = lax.all_to_all(outgoing, ("z",) + ROW, split_axis=0, concat_axis=0, tiled=True)
    incoming = incoming.reshape(owners, capacity, occupied, rows)
    return jnp.transpose(incoming, (1, 2, 0, 3)).reshape(capacity, occupied, owners * rows)


def solution(mesh):
    fine = Mesh(mesh.devices.reshape(8, 4, 2, 2, 2), ("z", "y", "xl", "xh", "core"))
    placed = (P(None, ("z", "y", "xl"), VIR), P(), P(), P(), P())
    return jax.shard_map(
        per_device,
        mesh=fine,
        in_specs=placed,
        out_specs=P(("z", "y", "xl", "xh", "core"), None, None),
        check_vma=False,
    )
```

time: 375 us -> 158 us (0.42)
  waiting for transfers between devices: 275 us -> 0 us
  Pallas kernels: 0 us -> 85.2 us
  between operations: 13.2 us -> 0.08 us
  matrix products: 19.4 us -> 7.09 us
    all_gather x2 -> x0, waiting for transfers between devices: 106 us -> none  [the longest x1 63.3 us: per_device(): row_block = lax.all_gather(factors, ROW, axis=1, tiled=True)]
    reduce_scatter x1 -> x0, waiting for transfers between devices: 100 us -> none  [per_device(): lax.psum_scatter(partial, ROW, scatter_dimension=1, tiled=True)]
    pallas_call x0 -> x1, Pallas kernels: none -> 85.2 us  [own_gamma(): pl.pallas_call(gamma_kernel, out_shape=jax.ShapeDtypeStruct((occupied, ro...]
    psum x1 -> x0, waiting for transfers between devices: 67.3 us -> none  [per_device(): pair = lax.psum(pair.reshape(-1), VIR).reshape(pair.shape)]
    dot_general x3 -> x1, matrix products: 19.4 us -> 7.09 us  [per_device(): jnp.einsum('sp,iap->sia', chosen, gamma, preferred_element_type=F32)]
  transfers between devices with their start and end apart: 4 -> 0, of which waited for: 4 -> 0; matrix products, arithmetic and copies ran while one was open for 0% -> 0% of each run, Pallas kernels for 0% -> 0%
where the time goes in v2:
time: 158 us; the launch traced here: 156 us
  Pallas kernels  85.2 us (54%)
  blocking collectives  27.8 us (18%)
  local copies, waits for them, and re-layouts  24.6 us (16%)
  other arithmetic  11.4 us (7%)
  matrix products  7.09 us (4%)
    pallas_call x1, Pallas kernels, own_gamma(): pl.pallas_call(gamma_kernel, out_shape=jax.ShapeDtypeStruct((occupied, ro...  85.2 us
    all_to_all x1, blocking collectives, per_device(): lax.all_to_all(outgoing, ('z',) + ROW, split_axis=0, concat_axis=0, tiled...  27.8 us
    all_to_all x2, other arithmetic, per_device(): lax.all_to_all(outgoing, ('z',) + ROW, split_axis=0, concat_axis=0, tiled...  11.1 us
    reshape x2, local copies, waits for them, and re-layouts, per_device(): jnp.transpose(incoming, (1, 2, 0, 3))  9.72 us
    dot_general x1, matrix products, per_device(): jnp.einsum('sp,iap->sia', chosen, gamma, preferred_element_type=F32)  7.09 us
    all_to_all x2, local copies, waits for them, and re-layouts, per_device(): lax.all_to_all(outgoing, ('z',) + ROW, split_axis=0, concat_axis=0, tiled...  4.89 us

profile of v2, /device:TPU:1, one launch (start us, length us, event | category | flops | bytes accessed | tf_op | source)
XLA Modules:
  0.0 156.2 jit_solution(4721202295351346428)
XLA Ops:
  0.0 0.7 fusion.7
  0.7 0.1 select_reduce_fusion.1
  0.8 0.8 reshape.56
  1.6 0.8 dynamic_slice.16
  2.4 0.1 select_reduce_fusion.2
  2.5 0.1 add_select_fusion
  2.6 0.1 select_n.38
  2.7 0.7 reshape.57.col_e_ref
  3.4 0.8 reshape.61.row_e_ref
  4.1 85.2 %own_gamma.1 = bf16[2,48,1536]{2,1,0:T(8,128)(2,1)} custom-call(bf16[2,48,1536]{2,1,0:T(8,128)(2,1)} %f_ref.1, f32[2]{0:T(128)} %occ_ref.1, f32[384,1]{1,0:T(8,128)} %reshape.61.row_e_ref, f32[1,384]{1,0:T(1,128)} %reshape.57.col_e_ref), custom_call_target="tpu_custom_call" | custom-call | tf_op jit(solution)/shard_map/own_gamma/pallas_call | solution.py:229
  89.4 7.1 %fusion.4 = bf16[4096,2,48]{0,2,1:T(8,128)(2,1)S(1)} fusion(bf16[2,48,1536]{2,1,0:T(8,128)(2,1)} %own_gamma.1, s32[4096]{0:T(1024)S(1)} %select_n.38), kind=kOutput, calls=%fused_computation.4 | convolution fusion | flops 1214644224 | bytes 1097728 | tf_op jit(solution)/shard_map/sp,iap->sia/dot_general | solution.py:274
  96.5 2.8 %copy.16 = bf16[4096,2,48]{2,1,0:T(2,128)(2,1)S(1)} copy(bf16[4096,2,48]{0,2,1:T(8,128)(2,1)S(1)} %fusion.4) | data formatting | bytes 1572864 | tf_op jit(solution)/shard_map/convert_element_type | solution.py:274
  99.3 4.4 %all_to_all.8 = bf16[64,1,6144]{2,1,0:T(2,128)(2,1)} reshape(bf16[4096,2,48]{2,1,0:T(2,128)(2,1)S(1)} %copy.16) | data formatting | bytes 1572864 | tf_op jit(solution)/shard_map/all_to_all | solution.py:276
  103.7 0.5 broadcast.21
  104.2 6.4 %reduce.5 = bf16[64,6144]{1,0:T(8,128)(2,1)S(1)} reduce(bf16[64,1,6144]{2,1,0:T(2,128)(2,1)} %all_to_all.8, bf16[]{:T(256)} %broadcast.21), dimensions={1}, to_apply=%all_to_all.8.reduce_sub_computation | reduce | bytes 1572866 | tf_op jit(solution)/shard_map/all_to_all | solution.py:276
  110.6 0.6 reshape.71
  111.2 27.8 %all_to_all.10 = bf16[64,2,3072]{2,1,0:T(2,128)(2,1)S(1)} all-to-all(bf16[64,2,3072]{2,1,0:T(2,128)(2,1)S(1)} %reshape.71), channel_id=1, replica_groups=mesh['z'=8,'y'=4,'xl'=2,'xh'=2,'core'=2] {'z','y','xl'}, dimensions={0} | all-to-all | bytes 1572864 | tf_op jit(solution)/shard_map/all_to_all | solution.py:276
  139.0 0.6 reshape.72
  139.6 4.7 %reduce.1 = bf16[64,6144]{1,0:T(8,128)(2,1)S(1)} reduce(bf16[64,1,6144]{2,1,0:T(2,128)(2,1)S(1)} %reshape.72, bf16[]{:T(256)} %constant.43), dimensions={1}, to_apply=%all_to_all.7.reduce_sub_computation | reduce | bytes 1572866 | tf_op jit(solution)/shard_map/all_to_all | solution.py:276
  144.3 2.2 %reshape.58 = bf16[64,64,2,48]{3,2,1,0:T(2,128)(2,1)S(1)} reshape(bf16[64,6144]{1,0:T(8,128)(2,1)S(1)} %reduce.1) | data formatting | bytes 1572864 | tf_op jit(solution)/shard_map/reshape | solution.py:277
  146.5 3.8 %copy.20 = bf16[64,2,64,48]{3,2,1,0:T(8,128)(2,1)} copy(bf16[64,2,64,48]{3,1,0,2:T(2,128)(2,1)S(1)} %bitcast.13) | data formatting | bytes 1572864 | tf_op jit(solution)/shard_map/reshape | solution.py:278
  150.3 5.9 %reshape.62 = bf16[64,2,3072]{2,1,0:T(2,128)(2,1)} reshape(bf16[64,2,64,48]{3,2,1,0:T(8,128)(2,1)} %copy.20) | data formatting | bytes 1572864 | tf_op jit(solution)/shard_map/reshape | solution.py:278
  (1 shorter events, 0.0 us)

commit v3 on v2

--- a/solution.py
+++ b/solution.py
@@ -21,20 +21,27 @@
 
 
 def gamma_kernel(
-    f_ref, occ_ref, row_e_ref, col_e_ref, out_ref,
+    f_ref, occ_ref, row_e_ref, col_e_ref, cols_ref, out_ref,
     rbuf, cbuf, m_send, m_own, m_recv, h_send, h_recv, abuf, part,
     a_send, a_recv, b_send, b_recv, x_out, x_recv,
+    hop, chosen, gamma, pick_out, pick_in, turned,
     zs, zr, ys, yr, xs, xr, ms, mr, hs, hr, as_, ar, pas, par, pbs, pbr, pxs, pxr,
+    rs, rr, qs, qr, ts, tr,
 ):
     z, y, xl, xh, core = (lax.axis_index(n) for n in ("z", "y", "xl", "xh", "core"))
     rows = f_ref.shape[1]
     width = f_ref.shape[2]
 
     barrier = pltpu.get_barrier_semaphore()
-    peers = [
-        {"z": ring("z", 1)}, {"z": ring("z", -1)}, {"y": ring("y", 1)}, {"y": ring("y", -1)},
-        {"xl": flip("xl")}, {"xh": flip("xh")}, {"core": flip("core")},
-    ]
+    yx_steps = [(2, True), (2, False), (1, True), (-1, True), (1, False), (-1, False), (0, True)]
+    yx_peers = [{"y": ring("y", dy), "xl": flip("xl") if other else xl} for dy, other in yx_steps]
+    z_steps = (4, 3, -3, 2, -2, 1, -1)
+    z_peers = [{"z": ring("z", dz)} for dz in z_steps]
+    core_to = {"core": flip("core")}
+    pair_to = {"xl": flip("xl")}
+    cross_to = {"xh": flip("xh"), "xl": flip("xl")}
+    xh_to = {"xh": flip("xh")}
+    peers = yx_peers + z_peers + [core_to, cross_to, xh_to]
     for peer in peers:
         pl.semaphore_signal(barrier, inc=1, device_id=peer, device_id_type=pl.DeviceIdType.MESH)
     pl.semaphore_wait(barrier, len(peers))
@@ -94,6 +101,15 @@
     for i in (0, 1):
         cbuf[i, z] = f_ref[i]
         rbuf[i, yx(0, False)] = f_ref[i]
+    def choose(step, carry):
+        block = step // 6
+        first = pl.multiple_of(lax.rem(step, 6) * (width // 6), width // 6)
+        at = lax.broadcasted_iota(jnp.int32, (width // 6, cols_ref.shape[2]), 0) + first
+        hit = at == cols_ref[block]
+        chosen[block, pl.ds(first, width // 6), :] = jnp.where(hit, 1.0, 0.0).astype(BF16)
+        return carry
+
+    lax.fori_loop(0, 8 * 6, choose, 0)
     for d in (0, 1):
         z_arrive(d, 1, 0)
         z_send(d, 2, 0)
@@ -145,21 +161,22 @@
         lhs = rbuf[i, pl.ds(h * 4, 4)].reshape(half, width)
         return lax.dot_general(lhs, columns, (((1,), (1,)), ((), ())), preferred_element_type=F32)
 
-    core_to = {"core": flip("core")}
     for i in (0, 1):
         m_send[i] = pair_rows(i, 1 - core)
         send(m_send.at[i], m_recv.at[i], ms.at[i], mr.at[i], core_to)
     for i in (0, 1):
         m_own[i] = pair_rows(i, core)
-    xh_to = {"xh": flip("xh")}
     for i in (0, 1):
         arrive(m_recv.at[i], mr.at[i])
         total = m_own[i] + m_recv[i]
         m_own[i] = total
         h_send[i] = total.astype(BF16)
-        send(h_send.at[i], h_recv.at[i], hs.at[i], hr.at[i], xh_to)
-    for i in (0, 1):
-        arrive(h_recv.at[i], hr.at[i])
+        send(h_send.at[i], hop.at[i], hs.at[i], hr.at[i], (pair_to, cross_to)[i])
+    for i in (0, 1):
+        arrive(hop.at[i], hr.at[i])
+        send(hop.at[i], h_recv.at[i], rs.at[i], rr.at[i], (cross_to, pair_to)[i])
+    for i in (0, 1):
+        arrive(h_recv.at[i], rr.at[i])
         m_own[i] = m_own[i] + h_recv[i].astype(F32)
     row_e = row_e_ref[pl.ds(pl.multiple_of(core * half, 16), half), :]
     col_e = col_e_ref[...]
@@ -208,12 +225,39 @@
     for i in (0, 1):
         near = part[0, i, own_rows] + b_recv[0, i, own_rows].astype(F32) + b_recv[1, i, own_rows].astype(F32)
         arrive(x_recv.at[i], pxr.at[i])
-        out_ref[i] = (near + x_recv[i].astype(F32)).astype(BF16)
+        gamma[pl.ds(i * rows, rows), :] = (near + x_recv[i].astype(F32)).astype(BF16)
+
+    slots = cols_ref.shape[2]
+    me = yx(0, False)
+
+    def picked(block):
+        got = jnp.dot(gamma[...], chosen[block], preferred_element_type=F32)
+        return got.astype(BF16).reshape(2, rows, slots)
+
+    for k, (dy, other) in enumerate(yx_steps):
+        pick_out[k] = picked(yx(dy, other))
+        send(pick_out.at[k], pick_in.at[:, me], qs.at[k], qr.at[k], yx_peers[k])
+    pick_in[:, me] = picked(me)
+    for k, (dy, other) in enumerate(yx_steps):
+        arrive(pick_in.at[:, yx(-dy, other)], qr.at[k])
+    for c in range(slots // 128):
+        block = pick_in[:, :, :, pl.ds(c * 128, 128)].reshape(2 * side, 128)
+        turned[pl.ds(c * 128, 128), :] = block.astype(F32).T.astype(BF16)
+    capacity = slots // 8
+
+    def owner_rows(dz):
+        return turned.at[pl.ds(pl.multiple_of(ring("z", dz) * capacity, 16), capacity)]
+
+    for k, dz in enumerate(z_steps):
+        send(owner_rows(dz), out_ref.at[z], ts.at[k], tr.at[k], z_peers[k])
+    out_ref[z] = owner_rows(0)[...]
+    for k, dz in enumerate(z_steps):
+        arrive(out_ref.at[ring("z", -dz)], tr.at[k])
     for copy in started:
         copy.wait_send()
 
 
-def own_gamma(factors, occ_energy, vir_energy):
+def owned_columns(factors, occ_energy, vir_energy, columns):
     occupied, rows, width = factors.shape
     nz, nyx = lax.axis_size("z"), lax.axis_size(ROW)
     group = rows * nyx
@@ -225,11 +269,12 @@
     dma = pltpu.SemaphoreType.DMA
     vmem = pl.BlockSpec(memory_space=pltpu.VMEM)
     smem = pl.BlockSpec(memory_space=pltpu.SMEM)
-    sems = [(2, 4, 2)] * 2 + [(2, 4)] * 2 + [(6,)] * 2 + [(2,)] * 8 + [(2, 2)] * 2 + [(2,)] * 2
+    sems = [(2, 4, 2)] * 2 + [(2, 4)] * 2 + [(6,)] * 2 + [(2,)] * 8 + [(2, 2)] * 2 + [(2,)] * 4 + [(7,)] * 4
+    slots = columns.shape[1]
     return pl.pallas_call(
         gamma_kernel,
-        out_shape=jax.ShapeDtypeStruct((occupied, rows, width), BF16),
-        in_specs=[vmem, smem, vmem, vmem],
+        out_shape=jax.ShapeDtypeStruct((nz, slots // nz, 2 * group), BF16),
+        in_specs=[vmem, smem, vmem, vmem, vmem],
         out_specs=vmem,
         scratch_shapes=[
             pltpu.VMEM((2, nyx, rows, width), BF16),
@@ -247,12 +292,18 @@
             pltpu.VMEM((2, 2, 2 * rows, width), BF16),
             pltpu.VMEM((2, rows, width), BF16),
             pltpu.VMEM((2, rows, width), BF16),
+            pltpu.VMEM((2, half, 2 * group), BF16),
+            pltpu.VMEM((nyx, width, slots), BF16),
+            pltpu.VMEM((2 * rows, width), BF16),
+            pltpu.VMEM((7, 2, rows, slots), BF16),
+            pltpu.VMEM((2, nyx, rows, slots), BF16),
+            pltpu.VMEM((slots, 2 * group), BF16),
         ] + [dma(s) for s in sems],
         compiler_params=pltpu.CompilerParams(
             collective_id=0, has_side_effects=True, vmem_limit_bytes=56 * 1024 * 1024
         ),
-        name="own_gamma",
-    )(factors, occ_energy, row_e, col_e)
+        name="owned_columns",
+    )(factors, occ_energy, row_e, col_e, columns.reshape(nyx, 1, slots))
 
 
 def per_device(factors, occ_energy, vir_energy, block_lengths, block_owner):
@@ -269,13 +320,11 @@
     dest_length = jnp.sum(jnp.where(match, lengths[None, :], 0), axis=1)
     slot = jnp.arange(capacity, dtype=jnp.int32)
     columns = jnp.where(slot[None, :] < dest_length[:, None], dest_start[:, None] + slot[None, :], -1)
-    gamma = own_gamma(factors, occ_energy, vir_energy)
-    chosen = (columns.reshape(-1)[:, None] == jnp.arange(width, dtype=jnp.int32)[None, :]).astype(BF16)
-    picked = jnp.einsum("sp,iap->sia", chosen, gamma, preferred_element_type=F32).astype(BF16)
-    outgoing = picked.reshape(owners, capacity * occupied * rows)
-    incoming = lax.all_to_all(outgoing, ("z",) + ROW, split_axis=0, concat_axis=0, tiled=True)
-    incoming = incoming.reshape(owners, capacity, occupied, rows)
-    return jnp.transpose(incoming, (1, 2, 0, 3)).reshape(capacity, occupied, owners * rows)
+    nz, nyx = lax.axis_size("z"), lax.axis_size(ROW)
+    columns = jnp.transpose(columns.reshape(nz, nyx, capacity), (1, 0, 2)).reshape(nyx, nz * capacity)
+    got = owned_columns(factors, occ_energy, vir_energy, columns)
+    got = got.reshape(nz, capacity, occupied, nyx * rows)
+    return jnp.transpose(got, (1, 2, 0, 3)).reshape(capacity, occupied, owners * rows)
 
 
 def solution(mesh):

time: 158 us -> 128 us (0.81); the launches traced: 156 us -> 128 us
  Pallas kernels: 85.2 us -> 121 us
  blocking collectives: 27.8 us -> 0 us
  local copies, waits for them, and re-layouts: 24.6 us -> 6.55 us
  other arithmetic: 11.4 us -> 0.85 us
  matrix products: 7.09 us -> 0 us
    pallas_call x1, Pallas kernels: 85.2 us -> 121 us  [owned_columns(): pl.pallas_call(gamma_kernel, out_shape=jax.ShapeDtypeStruct((nz, slots //...]
    all_to_all x1 -> x0, blocking collectives: 27.8 us -> none  [per_device(): lax.all_to_all(outgoing, ('z',) + ROW, split_axis=0, concat_axis=0, tiled...]
    all_to_all x2 -> x0, other arithmetic: 11.1 us -> none  [per_device(): lax.all_to_all(outgoing, ('z',) + ROW, split_axis=0, concat_axis=0, tiled...]
    reshape x6 -> x5, local copies, waits for them, and re-layouts: 14.2 us -> 5.01 us  [the longest x1 2.06 us: per_device(): got = got.reshape(nz, capacity, occupied, nyx * rows)]
    dot_general x1 -> x0, matrix products: 7.09 us -> none  [per_device(): jnp.einsum('sp,iap->sia', chosen, gamma, preferred_element_type=F32)]
    all_to_all x2 -> x0, local copies, waits for them, and re-layouts: 4.89 us -> none  [per_device(): lax.all_to_all(outgoing, ('z',) + ROW, split_axis=0, concat_axis=0, tiled...]
    convert_element_type x1 -> x0, local copies, waits for them, and re-layouts: 2.8 us -> none  [per_device(): jnp.einsum('sp,iap->sia', chosen, gamma, preferred_element_type=F32)]
where the time goes in v3:
time: 128 us
  Pallas kernels  121 us (95%)
  local copies, waits for them, and re-layouts  6.55 us (5%)
    pallas_call x1, Pallas kernels, owned_columns(): pl.pallas_call(gamma_kernel, out_shape=jax.ShapeDtypeStruct((nz, slots //...  121 us

profile of v3, /device:TPU:1, one launch (start us, length us, event | category | flops | bytes accessed | tf_op | source)
XLA Modules:
  0.0 128.2 jit_solution(2664742141492821348)
XLA Ops:
  0.0 0.0 copy-start
  0.0 0.7 fusion
  0.7 0.1 select_reduce_fusion.1
  0.8 0.1 select_reduce_fusion
  0.9 0.0 copy-done
  1.0 0.1 dynamic_slice.14
  1.0 0.1 add.47
  1.1 0.1 copy.14
  1.2 0.1 lt.65
  1.3 0.1 copy.13
  1.3 0.1 lt.62
  1.4 0.1 lt.67
  1.5 0.1 lt.68
  1.6 0.1 add.49
  1.7 0.1 add.50
  1.8 0.6 compare_select_fusion.cols_ref
  2.4 0.1 reshape.87
  2.5 0.7 reshape.88.col_e_ref
  3.2 0.8 reshape.91.row_e_ref
  4.0 120.7 %owned_columns.1 = bf16[8,64,768]{2,1,0:T(8,128)(2,1)} custom-call(bf16[2,48,1536]{2,1,0:T(8,128)(2,1)} %f_ref.1, f32[2]{0:T(128)} %occ_ref.1, f32[384,1]{1,0:T(8,128)} %reshape.91.row_e_ref, f32[1,384]{1,0:T(1,128)} %reshape.88.col_e_ref, s32[8,1,512]{2,1,0:T(1,128)} %compare_select_fusion.cols_ref), custom_call_target="tpu_custom_call" | custom-call | tf_op jit(solution)/shard_map/owned_columns/pallas_call | solution.py:274
  124.7 2.1 %reshape.89 = bf16[8,64,2,384]{3,2,1,0:T(2,128)(2,1)S(1)} reshape(bf16[8,64,768]{2,1,0:T(8,128)(2,1)} %owned_columns.1) | data formatting | bytes 1572864 | tf_op jit(solution)/shard_map/reshape | solution.py:326
  126.8 1.4 %copy.17 = bf16[8,64,1,2,384]{4,3,0,2,1:T(2,128)(2,1)} copy(bf16[8,64,1,2,384]{4,3,2,1,0:T(2,128)(2,1)S(1)} %bitcast.9) | data formatting | bytes 1572864 | tf_op jit(solution)/shard_map/reshape | solution.py:327
  (2 shorter events, 0.0 us)
Async XLA Ops:
  0.0 0.9 copy-start

commit v4 on v2

v4 whole, which is shorter than its diff:
```python
import jax
import jax.numpy as jnp
from jax import lax
from jax.experimental import pallas as pl
from jax.experimental.pallas import tpu as pltpu
from jax.sharding import Mesh, PartitionSpec as P

ROW = ("y", "xl")
VIR = ("xh", "core")
F32 = jnp.float32
BF16 = jnp.bfloat16


def ring(axis, shift):
    n = lax.axis_size(axis)
    return lax.rem(lax.axis_index(axis) + shift + n, n)


def flip(axis):
    return 1 - lax.axis_index(axis)


def gamma_kernel(
    f_ref, occ_ref, vir_ref, start_ref, length_ref, out_ref,
    rbuf, cbuf, m_send, m_own, m_recv, h_send, h_recv, hop, abuf, part, row_e_buf,
    ya_out, ya_in, yb_out, yb_in, yc_out, yc_in, xa_out, xa_in, xb_out, xb_in, xc_out, xc_in,
    chosen, gamma, pick_out, pick_in, turned,
    zs, zr, ys, yr, xs, xr, ms, mr, hs, hr, rs, rr, as_, ar,
    yas, yar, ybs, ybr, ycs, ycr, xas, xar, xbs, xbr, xcs, xcr, qs, qr, ts, tr,
):
    z, y, xl, xh, core = (lax.axis_index(n) for n in ("z", "y", "xl", "xh", "core"))
    rows = f_ref.shape[1]
    width = f_ref.shape[2]

    barrier = pltpu.get_barrier_semaphore()
    yx_steps = [(2, True), (2, False), (1, True), (-1, True), (1, False), (-1, False), (0, True)]
    yx_peers = [{"y": ring("y", dy), "xl": flip("xl") if other else xl} for dy, other in yx_steps]
    z_steps = (4, 3, -3, 2, -2, 1, -1)
    z_peers = [{"z": ring("z", dz)} for dz in z_steps]
    core_to = {"core": flip("core")}
    pair_to = {"xl": flip("xl")}
    cross_to = {"xh": flip("xh"), "xl": flip("xl")}
    xh_to = {"xh": flip("xh")}
    peers = yx_peers + z_peers + [core_to, cross_to, xh_to]
    for peer in peers:
        pl.semaphore_signal(barrier, inc=1, device_id=peer, device_id_type=pl.DeviceIdType.MESH)
    pl.semaphore_wait(barrier, len(peers))

    started = []

    def send(src, dst, ssem, rsem, peer):
        copy = pltpu.make_async_remote_copy(
            src_ref=src, dst_ref=dst, send_sem=ssem, recv_sem=rsem,
            device_id=peer, device_id_type=pl.DeviceIdType.MESH,
        )
        copy.start()
        started.append(copy)
        return copy

    def arrive(dst, rsem):
        pltpu.make_async_remote_copy(
            src_ref=dst, dst_ref=dst, send_sem=rsem, recv_sem=rsem,
            device_id=peers[0], device_id_type=pl.DeviceIdType.MESH,
        ).wait_recv()

    def yx(dy, other):
        return ring("y", dy) * 2 + (flip("xl") if other else xl)

    z_to = ({"z": ring("z", 1)}, {"z": ring("z", -1)})
    y_to = ({"y": ring("y", 1)}, {"y": ring("y", -1)})
    x_to = {"xl": flip("xl")}

    def z_send(d, step, i):
        origin = ring("z", (1 - step) if d == 0 else (step - 1))
        src = f_ref.at[i] if step == 1 else cbuf.at[i, origin]
        send(src, cbuf.at[i, origin], zs.at[d, step - 1, i], zr.at[d, step - 1, i], z_to[d])

    def z_arrive(d, step, i):
        origin = ring("z", -step if d == 0 else step)
        arrive(cbuf.at[i, origin], zr.at[d, step - 1, i])

    def y_send(d, k, i, dy, other):
        src = f_ref.at[i] if (dy == 0 and not other) else rbuf.at[i, yx(dy, other)]
        send(src, rbuf.at[i, yx(dy, other)], ys.at[d, k], yr.at[d, k], y_to[d])

    def y_arrive(d, k, i, dy, other):
        arrive(rbuf.at[i, yx(dy, other)], yr.at[d, k])

    def x_send(k, i, dy):
        src = f_ref.at[i] if dy == 0 else rbuf.at[i, yx(dy, False)]
        send(src, rbuf.at[i, yx(dy, False)], xs.at[k], xr.at[k], x_to)

    def x_arrive(k, i, dy):
        arrive(rbuf.at[i, yx(dy, True)], xr.at[k])

    for i in (0, 1):
        for d in (0, 1):
            z_send(d, 1, i)
            y_send(d, i, i, 0, False)
        x_send(i, i, 0)
    for i in (0, 1):
        cbuf[i, z] = f_ref[i]
        rbuf[i, yx(0, False)] = f_ref[i]
    slots = chosen.shape[2]
    capacity = slots // 8
    piece = width // 6

    def choose(block, carry):
        lane = lax.broadcasted_iota(jnp.int32, (1, slots), 1)
        first = jnp.zeros((1, slots), jnp.int32)
        count = jnp.zeros((1, slots), jnp.int32)
        for zt in range(8):
            here = lane // capacity == zt
            first = jnp.where(here, start_ref[zt * 8 + block], first)
            count = jnp.where(here, length_ref[zt * 8 + block], count)
        slot = lane % capacity
        column = jnp.where(slot < count, first + slot, -1)
        for k in range(6):
            at = lax.broadcasted_iota(jnp.int32, (piece, slots), 0) + k * piece
            chosen[block, pl.ds(k * piece, piece), :] = jnp.where(at == column, 1.0, 0.0).astype(BF16)
        return carry

    lax.fori_loop(0, 8, choose, 0)
    near_e = jnp.concatenate([vir_ref[pl.ds(z * 8 + k, 1), :] for k in range(8)], axis=1)
    row_e_buf[...] = jnp.broadcast_to(near_e, (128, 8 * rows)).T
    col_e = jnp.concatenate([vir_ref[pl.ds(k * 8 + yx(0, False), 1), :] for k in range(8)], axis=1)
    for d in (0, 1):
        z_arrive(d, 1, 0)
        z_send(d, 2, 0)
    y_arrive(0, 0, 0, -1, False)
    x_send(2, 0, -1)
    y_send(0, 2, 0, -1, False)
    y_arrive(1, 0, 0, 1, False)
    for d in (0, 1):
        z_arrive(d, 1, 1)
        z_send(d, 2, 1)
    y_arrive(1, 1, 1, 1, False)
    x_send(3, 1, 1)
    y_send(1, 2, 1, 1, False)
    x_send(4, 0, 1)
    y_arrive(0, 1, 1, -1, False)
    x_send(5, 1, -1)
    for d in (0, 1):
        z_arrive(d, 2, 0)
        z_send(d, 3, 0)
    x_arrive(0, 0, 0)
    x_arrive(1, 1, 0)
    x_arrive(2, 0, -1)
    y_send(0, 3, 0, -1, True)
    for d in (0, 1):
        z_arrive(d, 2, 1)
        z_send(d, 3, 1)
    x_arrive(3, 1, 1)
    y_send(1, 3, 1, 1, True)
    z_arrive(0, 3, 0)
    z_send(0, 4, 0)
    z_arrive(1, 3, 1)
    z_send(1, 4, 1)
    z_arrive(1, 3, 0)
    z_arrive(0, 3, 1)
    y_arrive(0, 2, 0, -2, False)
    y_arrive(1, 2, 1, 2, False)
    x_arrive(4, 0, 1)
    x_arrive(5, 1, -1)
    y_arrive(0, 3, 0, -2, True)
    y_arrive(1, 3, 1, 2, True)
    z_arrive(0, 4, 0)
    z_arrive(1, 4, 1)

    half = 4 * rows
    side = 8 * rows
    columns = cbuf[...].reshape(2 * side, width)

    def pair_rows(i, h):
        lhs = rbuf[i, pl.ds(h * 4, 4)].reshape(half, width)
        return lax.dot_general(lhs, columns, (((1,), (1,)), ((), ())), preferred_element_type=F32)

    for i in (0, 1):
        m_send[i] = pair_rows(i, 1 - core)
        send(m_send.at[i], m_recv.at[i], ms.at[i], mr.at[i], core_to)
    for i in (0, 1):
        m_own[i] = pair_rows(i, core)
    for i in (0, 1):
        arrive(m_recv.at[i], mr.at[i])
        total = m_own[i] + m_recv[i]
        m_own[i] = total
        h_send[i] = total.astype(BF16)
        send(h_send.at[i], hop.at[i], hs.at[i], hr.at[i], (pair_to, cross_to)[i])
    for i in (0, 1):
        arrive(hop.at[i], hr.at[i])
        send(hop.at[i], h_recv.at[i], rs.at[i], rr.at[i], (cross_to, pair_to)[i])
    for i in (0, 1):
        arrive(h_recv.at[i], rr.at[i])
        m_own[i] = m_own[i] + h_recv[i].astype(F32)
    row_e = row_e_buf[pl.ds(pl.multiple_of(core * half, 16), half), 0:1]
    mine = pl.ds(pl.multiple_of(core * half, 16), half)
    for i in (0, 1):
        for j in (0, 1):
            denominator = (occ_ref[i] + occ_ref[j]) - row_e - col_e
            direct = m_own[i, :, pl.ds(j * side, side)]
            swapped = m_own[j, :, pl.ds(i * side, side)]
            abuf[i, mine, pl.ds(j * side, side)] = ((2.0 * direct - swapped) / denominator).astype(BF16)
        send(abuf.at[i, mine], abuf.at[i, mine], as_.at[i], ar.at[i], core_to)
    theirs = pl.ds(pl.multiple_of((1 - core) * half, 16), half)
    for i in (0, 1):
        arrive(abuf.at[i, theirs], ar.at[i])

    cols = width // 2
    quad = cols // 2
    me = yx(0, False)
    mate = yx(0, True)
    left, right = pl.ds(0, cols), pl.ds(cols, cols)

    def wide(ref):
        return ref[...].astype(F32)

    def product(i):
        for h in (0, 1):
            lhs = abuf[i, pl.ds(h * half, half)]
            res = jnp.dot(lhs, cbuf[...].reshape(2 * side, width), preferred_element_type=F32)
            part[i, pl.ds(4 * h, 4)] = res.reshape(4, rows, width)

    def s1(i):
        for d in (0, 1):
            ya_out[i, d] = part[i, ring("y", 2) * 2 + d, :, left].astype(BF16)
            send(ya_out.at[i, d], ya_in.at[i, d], yas.at[i, d], yar.at[i, d], y_to[d])
        for k, dy in enumerate((2, 1, -1, 0)):
            xa_out[i, k] = part[i, yx(dy, True), :, right].astype(BF16)
            send(xa_out.at[i, k], xa_in.at[i, k], xas.at[i, k], xar.at[i, k], x_to)
        for d in (0, 1):
            yb_send(i, d, 1 - d, part[i, ring("y", 1 - 2 * d) * 2 + 1 - d, :, left])

    def yb_send(i, d, e, value):
        yb_out[i, d, e] = value.astype(BF16)
        send(yb_out.at[i, d, e], yb_in.at[i, d, e], ybs.at[i, d, e], ybr.at[i, d, e], y_to[d])

    def s2(i):
        for d in (0, 1):
            arrive(ya_in.at[i, d], yar.at[i, d])
            yb_send(i, d, d, part[i, ring("y", 1 - 2 * d) * 2 + d, :, left] + wide(ya_in.at[i, d]))

    def xc_send(i, d, e, value):
        xc_out[i, d, e] = value.astype(BF16)
        send(xc_out.at[i, d, e], xc_in.at[i, d, e], xcs.at[i, d, e], xcr.at[i, d, e], y_to[d])

    def x_sum(i, k, dy, e):
        at = pl.ds(cols + e * quad, quad)
        return part[i, yx(dy, False), :, at] + xa_in[i, k, :, pl.ds(e * quad, quad)].astype(F32)

    def s3(i):
        arrive(xa_in.at[i, 0], xar.at[i, 0])
        for d in (0, 1):
            xb_out[i, d] = x_sum(i, 0, 2, d).astype(BF16)
            send(xb_out.at[i, d], xb_in.at[i, d], xbs.at[i, d], xbr.at[i, d], y_to[d])
        for d in (0, 1):
            arrive(xa_in.at[i, 1 + d], xar.at[i, 1 + d])
            xc_send(i, d, 1 - d, x_sum(i, 1 + d, 1 - 2 * d, 1 - d))

    def s4(i):
        for d in (0, 1):
            arrive(xb_in.at[i, d], xbr.at[i, d])
            xc_send(i, d, d, x_sum(i, 1 + d, 1 - 2 * d, d) + wide(xb_in.at[i, d]))

    def s5(i):
        for d in (0, 1):
            for e in (1 - d, d):
                arrive(yb_in.at[i, d, e], ybr.at[i, d, e])
        far = part[i, mate, :, left] + wide(yb_in.at[i, 0, 1 - xl]) + wide(yb_in.at[i, 1, 1 - xl])
        yc_out[i] = far.astype(BF16)
        send(yc_out.at[i], yc_in.at[i], ycs.at[i], ycr.at[i], x_to)

    def s6(i):
        arrive(xa_in.at[i, 3], xar.at[i, 3])
        for d in (0, 1):
            for e in (1 - d, d):
                arrive(xc_in.at[i, d, e], xcr.at[i, d, e])
        for e in (0, 1):
            total = x_sum(i, 3, 0, e) + wide(xc_in.at[i, 0, e]) + wide(xc_in.at[i, 1, e])
            gamma[i, :, pl.ds(cols + e * quad, quad)] = total.astype(BF16)
        near = part[i, me, :, left] + wide(yb_in.at[i, 0, xl]) + wide(yb_in.at[i, 1, xl])
        arrive(yc_in.at[i], ycr.at[i])
        gamma[i, :, left] = (near + wide(yc_in.at[i])).astype(BF16)

    def picked(i, block):
        return jnp.dot(gamma[i], chosen[block], preferred_element_type=F32).astype(BF16)

    def s7(i):
        for k, (dy, other) in enumerate(yx_steps):
            pick_out[i, k] = picked(i, yx(dy, other))
            send(pick_out.at[i, k], pick_in.at[i, me], qs.at[i, k], qr.at[i, k], yx_peers[k])
        pick_in[i, me] = picked(i, me)

    def owner_rows(i, dz):
        return turned.at[i, pl.ds(pl.multiple_of(ring("z", dz) * capacity, 16), capacity)]

    def s8(i):
        for k, (dy, other) in enumerate(yx_steps):
            arrive(pick_in.at[i, yx(-dy, other)], qr.at[i, k])
        for c in range(slots // 128):
            block = pick_in[i, :, :, pl.ds(c * 128, 128)].reshape(side, 128)
            turned[i, pl.ds(c * 128, 128), :] = block.astype(F32).T.astype(BF16)
        for k, dz in enumerate(z_steps):
            send(owner_rows(i, dz), out_ref.at[i, z], ts.at[i, k], tr.at[i, k], z_peers[k])
        out_ref[i, z] = owner_rows(i, 0)[...]

    def s9(i):
        for k, dz in enumerate(z_steps):
            arrive(out_ref.at[i, ring("z", -dz)], tr.at[i, k])

    product(0)
    s1(0)
    product(1)
    s2(0)
    s3(0)
    s1(1)
    s4(0)
    s5(0)
    s2(1)
    s3(1)
    s6(0)
    s7(0)
    s4(1)
    s5(1)
    s8(0)
    s6(1)
    s7(1)
    s8(1)
    s9(0)
    s9(1)
    for copy in started:
        copy.wait_send()


def owned_columns(factors, occ_energy, vir_energy, start, length):
    occupied, rows, width = factors.shape
    nz, nyx = lax.axis_size("z"), lax.axis_size(ROW)
    group = rows * nyx
    half = group // 2
    slots = 8 * width // (3 * nyx)
    cols = width // 2
    dma = pltpu.SemaphoreType.DMA
    vmem = pl.BlockSpec(memory_space=pltpu.VMEM)
    smem = pl.BlockSpec(memory_space=pltpu.SMEM)
    wide = [pltpu.VMEM((2, half, 2 * group), F32)] * 3
    thin = [pltpu.VMEM((2, half, 2 * group), BF16)] * 3

    def pair_of(*shape):
        return [pltpu.VMEM(shape, BF16)] * 2

    sems = [(2, 4, 2)] * 2 + [(2, 4)] * 2 + [(6,)] * 2 + [(2,)] * 8
    sems += [(2, 2)] * 2 + [(2, 2, 2)] * 2 + [(2,)] * 2 + [(2, 4)] * 2 + [(2, 2)] * 2 + [(2, 2, 2)] * 2 + [(2, 7)] * 4
    return pl.pallas_call(
        gamma_kernel,
        out_shape=jax.ShapeDtypeStruct((2, nz, slots // nz, group), BF16),
        in_specs=[vmem, smem, vmem, smem, smem],
        out_specs=vmem,
        scratch_shapes=pair_of(2, 8, rows, width)
        + wide
        + thin
        + [
            pltpu.VMEM((2, group, 2 * group), BF16),
            pltpu.VMEM((2, nyx, rows, width), F32),
            pltpu.VMEM((group, 128), F32),
        ]
        + pair_of(2, 2, rows, cols)
        + pair_of(2, 2, 2, rows, cols)
        + pair_of(2, rows, cols)
        + pair_of(2, 4, rows, cols)
        + pair_of(2, 2, rows, cols // 2)
        + pair_of(2, 2, 2, rows, cols // 2)
        + [
            pltpu.VMEM((nyx, width, slots), BF16),
            pltpu.VMEM((2, rows, width), BF16),
            pltpu.VMEM((2, 7, rows, slots), BF16),
            pltpu.VMEM((2, nyx, rows, slots), BF16),
            pltpu.VMEM((2, slots, group), BF16),
        ]
        + [dma(s) for s in sems],
        compiler_params=pltpu.CompilerParams(
            collective_id=0, has_side_effects=True, vmem_limit_bytes=60 * 1024 * 1024
        ),
        name="owned_columns",
    )(factors, occ_energy, vir_energy.reshape(nz * nyx, rows), start, length)


def per_device(factors, occ_energy, vir_energy, block_lengths, block_owner):
    occupied, rows, width = factors.shape
    nz, nyx = lax.axis_size("z"), lax.axis_size(ROW)
    owners = nz * nyx
    quarter = lax.axis_index(VIR)
    lengths = lax.dynamic_index_in_dim(block_lengths, quarter, 0, keepdims=False)
    owner_of = lax.dynamic_index_in_dim(block_owner, quarter, 0, keepdims=False)
    order = jnp.arange(owners, dtype=jnp.int32)
    starts = jnp.sum(jnp.where(order[None, :] < order[:, None], lengths[None, :], 0), axis=1)
    match = owner_of[None, :] == order[:, None]
    dest_start = jnp.sum(jnp.where(match, starts[None, :], 0), axis=1)
    dest_length = jnp.sum(jnp.where(match, lengths[None, :], 0), axis=1)
    got = owned_columns(factors, occ_energy, vir_energy, dest_start, dest_length)
    return jnp.transpose(got, (2, 0, 1, 3)).reshape(got.shape[2], occupied, owners * rows)


def solution(mesh):
    fine = Mesh(mesh.devices.reshape(8, 4, 2, 2, 2), ("z", "y", "xl", "xh", "core"))
    placed = (P(None, ("z", "y", "xl"), VIR), P(), P(), P(), P())
    return jax.shard_map(
        per_device,
        mesh=fine,
        in_specs=placed,
        out_specs=P(("z", "y", "xl", "xh", "core"), None, None),
        check_vma=False,
    )
```

time: 158 us -> 111 us (0.70)
  blocking collectives: 27.8 us -> 0 us
  Pallas kernels: 85.2 us -> 106 us
  local copies, waits for them, and re-layouts: 24.6 us -> 4.06 us
  other arithmetic: 11.4 us -> 0.81 us
  matrix products: 7.09 us -> 0 us
    all_to_all x1 -> x0, blocking collectives: 27.8 us -> none  [per_device(): lax.all_to_all(outgoing, ('z',) + ROW, split_axis=0, concat_axis=0, tiled...]
    pallas_call x1, Pallas kernels: 85.2 us -> 106 us  [owned_columns(): pl.pallas_call(gamma_kernel, out_shape=jax.ShapeDtypeStruct((2, nz, slots...]
    all_to_all x2 -> x0, other arithmetic: 11.1 us -> none  [per_device(): lax.all_to_all(outgoing, ('z',) + ROW, split_axis=0, concat_axis=0, tiled...]
    reshape x6 -> x3, local copies, waits for them, and re-layouts: 14.2 us -> 3.34 us  [the longest x2 2.65 us: per_device(): jnp.transpose(got, (2, 0, 1, 3))]
    dot_general x1 -> x0, matrix products: 7.09 us -> none  [per_device(): jnp.einsum('sp,iap->sia', chosen, gamma, preferred_element_type=F32)]
    all_to_all x2 -> x0, local copies, waits for them, and re-layouts: 4.89 us -> none  [per_device(): lax.all_to_all(outgoing, ('z',) + ROW, split_axis=0, concat_axis=0, tiled...]
    convert_element_type x1 -> x0, local copies, waits for them, and re-layouts: 2.8 us -> none  [per_device(): jnp.einsum('sp,iap->sia', chosen, gamma, preferred_element_type=F32)]
where the time goes in v4:
time: 111 us
  Pallas kernels  106 us (95%)
  local copies, waits for them, and re-layouts  4.06 us (4%)
    pallas_call x1, Pallas kernels, owned_columns(): pl.pallas_call(gamma_kernel, out_shape=jax.ShapeDtypeStruct((2, nz, slots...  106 us
    reshape x2, local copies, waits for them, and re-layouts, per_device(): jnp.transpose(got, (2, 0, 1, 3))  2.65 us

profile of v4, /device:TPU:1, one launch (start us, length us, event | category | flops | bytes accessed | tf_op | source)
XLA Modules:
  0.0 110.8 jit_solution(10368644136531310382)
XLA Ops:
  0.0 0.0 copy-start
  0.0 0.7 dynamic-slice_bitcast_fusion
  0.7 0.1 select_reduce_fusion.2
  0.8 0.7 select_reduce_fusion
  1.5 0.0 copy-done
  1.5 0.7 reshape.7.vir_ref
  2.2 105.9 %owned_columns.1 = bf16[2,8,64,384]{3,2,1,0:T(8,128)(2,1)} custom-call(bf16[2,48,1536]{2,1,0:T(8,128)(2,1)} %f_ref.1, f32[2]{0:T(128)} %occ_ref.1, f32[64,48]{1,0:T(8,128)} %reshape.7.vir_ref, s32[64]{0:T(128)} %get-tuple-element.6.start_ref, s32[64]{0:T(128)} %get-tuple-element.5.length_ref), custom_call_target="tpu_custom_call" | custom-call | tf_op jit(solution)/shard_map/owned_columns/pallas_call | solution.py:352
  108.1 1.6 %copy.10 = bf16[64,2,8,384]{3,2,1,0:T(8,128)(2,1)S(1)} copy(bf16[64,2,8,384]{3,0,2,1:T(8,128)(2,1)} %bitcast.7) | data formatting | bytes 1572864 | tf_op jit(solution)/shard_map/reshape | solution.py:399
  109.7 1.1 reshape.9
Async XLA Ops:
  0.0 1.5 %copy-start = (f32[3072]{0:T(1024)S(1)}, f32[3072]{0:T(1024)}, u32[]{:S(2)}) copy-start(f32[3072]{0:T(1024)} %param.7) | copy-start | bytes 36868

commit v5 on v4

--- a/solution.py
+++ b/solution.py
@@ -24,9 +24,9 @@
     f_ref, occ_ref, vir_ref, start_ref, length_ref, out_ref,
     rbuf, cbuf, m_send, m_own, m_recv, h_send, h_recv, hop, abuf, part, row_e_buf,
     ya_out, ya_in, yb_out, yb_in, yc_out, yc_in, xa_out, xa_in, xb_out, xb_in, xc_out, xc_in,
-    chosen, gamma, pick_out, pick_in, turned,
+    gamma, window, spread, pick_out, pick_in, turned,
     zs, zr, ys, yr, xs, xr, ms, mr, hs, hr, rs, rr, as_, ar,
-    yas, yar, ybs, ybr, ycs, ycr, xas, xar, xbs, xbr, xcs, xcr, qs, qr, ts, tr,
+    yas, yar, ybs, ybr, ycs, ycr, xas, xar, xbs, xbr, xcs, xcr, qs, qr, ts, tr, fs, os_,
 ):
     z, y, xl, xh, core = (lax.axis_index(n) for n in ("z", "y", "xl", "xh", "core"))
     rows = f_ref.shape[1]
@@ -40,8 +40,7 @@
     core_to = {"core": flip("core")}
     pair_to = {"xl": flip("xl")}
     cross_to = {"xh": flip("xh"), "xl": flip("xl")}
-    xh_to = {"xh": flip("xh")}
-    peers = yx_peers + z_peers + [core_to, cross_to, xh_to]
+    peers = [z_peers[-2], z_peers[-1], yx_peers[4], yx_peers[5], pair_to, cross_to, core_to]
     for peer in peers:
         pl.semaphore_signal(barrier, inc=1, device_id=peer, device_id_type=pl.DeviceIdType.MESH)
     pl.semaphore_wait(barrier, len(peers))
@@ -98,29 +97,12 @@
             z_send(d, 1, i)
             y_send(d, i, i, 0, False)
         x_send(i, i, 0)
-    for i in (0, 1):
-        cbuf[i, z] = f_ref[i]
-        rbuf[i, yx(0, False)] = f_ref[i]
-    slots = chosen.shape[2]
-    capacity = slots // 8
-    piece = width // 6
-
-    def choose(block, carry):
-        lane = lax.broadcasted_iota(jnp.int32, (1, slots), 1)
-        first = jnp.zeros((1, slots), jnp.int32)
-        count = jnp.zeros((1, slots), jnp.int32)
-        for zt in range(8):
-            here = lane // capacity == zt
-            first = jnp.where(here, start_ref[zt * 8 + block], first)
-            count = jnp.where(here, length_ref[zt * 8 + block], count)
-        slot = lane % capacity
-        column = jnp.where(slot < count, first + slot, -1)
-        for k in range(6):
-            at = lax.broadcasted_iota(jnp.int32, (piece, slots), 0) + k * piece
-            chosen[block, pl.ds(k * piece, piece), :] = jnp.where(at == column, 1.0, 0.0).astype(BF16)
-        return carry
-
-    lax.fori_loop(0, 8, choose, 0)
+    local = []
+    for i in (0, 1):
+        local.append(pltpu.make_async_copy(f_ref.at[i], cbuf.at[i, z], fs.at[0, i]))
+        local.append(pltpu.make_async_copy(f_ref.at[i], rbuf.at[i, yx(0, False)], fs.at[1, i]))
+    for copy in local:
+        copy.start()
     near_e = jnp.concatenate([vir_ref[pl.ds(z * 8 + k, 1), :] for k in range(8)], axis=1)
     row_e_buf[...] = jnp.broadcast_to(near_e, (128, 8 * rows)).T
     col_e = jnp.concatenate([vir_ref[pl.ds(k * 8 + yx(0, False), 1), :] for k in range(8)], axis=1)
@@ -167,6 +149,9 @@
     z_arrive(0, 4, 0)
     z_arrive(1, 4, 1)
 
+    for copy in local:
+        copy.wait()
+
     half = 4 * rows
     side = 8 * rows
     columns = cbuf[...].reshape(2 * side, width)
@@ -214,21 +199,26 @@
     def wide(ref):
         return ref[...].astype(F32)
 
-    def product(i):
-        for h in (0, 1):
-            lhs = abuf[i, pl.ds(h * half, half)]
-            res = jnp.dot(lhs, cbuf[...].reshape(2 * side, width), preferred_element_type=F32)
-            part[i, pl.ds(4 * h, 4)] = res.reshape(4, rows, width)
+    slots = spread.shape[1]
+    capacity = slots // 8
+    thin = rows // 3
+    band = 8 * thin
+    window[pl.ds(width, capacity), :] = jnp.zeros((capacity, 128), F32)
+
+    def product(c):
+        lhs = abuf[:, pl.ds(c * band, band)].reshape(2 * band, 2 * side)
+        res = jnp.dot(lhs, cbuf[...].reshape(2 * side, width), preferred_element_type=F32)
+        part[c] = res.reshape(2, 8, thin, width)
 
     def s1(i):
         for d in (0, 1):
-            ya_out[i, d] = part[i, ring("y", 2) * 2 + d, :, left].astype(BF16)
+            ya_out[i, d] = part[i, :, ring("y", 2) * 2 + d, :, left].astype(BF16)
             send(ya_out.at[i, d], ya_in.at[i, d], yas.at[i, d], yar.at[i, d], y_to[d])
         for k, dy in enumerate((2, 1, -1, 0)):
-            xa_out[i, k] = part[i, yx(dy, True), :, right].astype(BF16)
+            xa_out[i, k] = part[i, :, yx(dy, True), :, right].astype(BF16)
             send(xa_out.at[i, k], xa_in.at[i, k], xas.at[i, k], xar.at[i, k], x_to)
         for d in (0, 1):
-            yb_send(i, d, 1 - d, part[i, ring("y", 1 - 2 * d) * 2 + 1 - d, :, left])
+            yb_send(i, d, 1 - d, part[i, :, ring("y", 1 - 2 * d) * 2 + 1 - d, :, left])
 
     def yb_send(i, d, e, value):
         yb_out[i, d, e] = value.astype(BF16)
@@ -237,7 +227,7 @@
     def s2(i):
         for d in (0, 1):
             arrive(ya_in.at[i, d], yar.at[i, d])
-            yb_send(i, d, d, part[i, ring("y", 1 - 2 * d) * 2 + d, :, left] + wide(ya_in.at[i, d]))
+            yb_send(i, d, d, part[i, :, ring("y", 1 - 2 * d) * 2 + d, :, left] + wide(ya_in.at[i, d]))
 
     def xc_send(i, d, e, value):
         xc_out[i, d, e] = value.astype(BF16)
@@ -245,7 +235,7 @@
 
     def x_sum(i, k, dy, e):
         at = pl.ds(cols + e * quad, quad)
-        return part[i, yx(dy, False), :, at] + xa_in[i, k, :, pl.ds(e * quad, quad)].astype(F32)
+        return part[i, :, yx(dy, False), :, at] + xa_in[i, k, :, :, pl.ds(e * quad, quad)].astype(F32)
 
     def s3(i):
         arrive(xa_in.at[i, 0], xar.at[i, 0])
@@ -265,9 +255,12 @@
         for d in (0, 1):
             for e in (1 - d, d):
                 arrive(yb_in.at[i, d, e], ybr.at[i, d, e])
-        far = part[i, mate, :, left] + wide(yb_in.at[i, 0, 1 - xl]) + wide(yb_in.at[i, 1, 1 - xl])
+        far = part[i, :, mate, :, left] + wide(yb_in.at[i, 0, 1 - xl]) + wide(yb_in.at[i, 1, 1 - xl])
         yc_out[i] = far.astype(BF16)
         send(yc_out.at[i], yc_in.at[i], ycs.at[i], ycr.at[i], x_to)
+
+    def rounded(total):
+        return total.astype(BF16).astype(F32).reshape(2 * thin, total.shape[2])
 
     def s6(i):
         arrive(xa_in.at[i, 3], xar.at[i, 3])
@@ -276,57 +269,82 @@
                 arrive(xc_in.at[i, d, e], xcr.at[i, d, e])
         for e in (0, 1):
             total = x_sum(i, 3, 0, e) + wide(xc_in.at[i, 0, e]) + wide(xc_in.at[i, 1, e])
-            gamma[i, :, pl.ds(cols + e * quad, quad)] = total.astype(BF16)
-        near = part[i, me, :, left] + wide(yb_in.at[i, 0, xl]) + wide(yb_in.at[i, 1, xl])
+            gamma[:, pl.ds(cols + e * quad, quad)] = rounded(total)
+        near = part[i, :, me, :, left] + wide(yb_in.at[i, 0, xl]) + wide(yb_in.at[i, 1, xl])
         arrive(yc_in.at[i], ycr.at[i])
-        gamma[i, :, left] = (near + wide(yc_in.at[i])).astype(BF16)
-
-    def picked(i, block):
-        return jnp.dot(gamma[i], chosen[block], preferred_element_type=F32).astype(BF16)
+        gamma[:, left] = rounded(near + wide(yc_in.at[i]))
+
+    row_at = lax.broadcasted_iota(jnp.int32, (capacity, 128), 0)
+
+    def picked(block):
+        for zt in range(8):
+            owner = zt * 8 + block
+            rows_of = window[pl.ds(start_ref[owner], capacity), :]
+            spread[0, pl.ds(zt * capacity, capacity), :] = jnp.where(row_at < length_ref[owner], rows_of, 0.0)
+        return spread[0].T[0 : 2 * thin].astype(BF16).reshape(2, thin, slots)
 
     def s7(i):
+        window[pl.ds(0, width), 0 : 2 * thin] = gamma[...].T
         for k, (dy, other) in enumerate(yx_steps):
-            pick_out[i, k] = picked(i, yx(dy, other))
+            pick_out[i, k] = picked(yx(dy, other))
             send(pick_out.at[i, k], pick_in.at[i, me], qs.at[i, k], qr.at[i, k], yx_peers[k])
-        pick_in[i, me] = picked(i, me)
+        pick_in[i, me] = picked(me)
 
     def owner_rows(i, dz):
-        return turned.at[i, pl.ds(pl.multiple_of(ring("z", dz) * capacity, 16), capacity)]
+        return turned.at[i, :, pl.ds(pl.multiple_of(ring("z", dz) * capacity, 16), capacity)]
+
+    def landing(i, dz):
+        return out_ref.at[:, :, pl.ds(pl.multiple_of(ring("z", dz) * side + i * band, 128), band)]
 
     def s8(i):
         for k, (dy, other) in enumerate(yx_steps):
             arrive(pick_in.at[i, yx(-dy, other)], qr.at[i, k])
-        for c in range(slots // 128):
-            block = pick_in[i, :, :, pl.ds(c * 128, 128)].reshape(side, 128)
-            turned[i, pl.ds(c * 128, 128), :] = block.astype(F32).T.astype(BF16)
+        for o in (0, 1):
+            for c in range(slots // 128):
+                block = pick_in[i, :, o, :, pl.ds(c * 128, 128)].reshape(band, 128)
+                turned[i, o, pl.ds(c * 128, 128), :] = block.astype(F32).T.astype(BF16)
         for k, dz in enumerate(z_steps):
-            send(owner_rows(i, dz), out_ref.at[i, z], ts.at[i, k], tr.at[i, k], z_peers[k])
-        out_ref[i, z] = owner_rows(i, 0)[...]
+            send(owner_rows(i, dz), landing(i, 0), ts.at[i, k], tr.at[i, k], z_peers[k])
+        own = pltpu.make_async_copy(owner_rows(i, 0), landing(i, 0), os_.at[i])
+        own.start()
+        kept.append(own)
 
     def s9(i):
         for k, dz in enumerate(z_steps):
-            arrive(out_ref.at[i, ring("z", -dz)], tr.at[i, k])
-
+            arrive(landing(i, -dz), tr.at[i, k])
+
+    kept = []
     product(0)
     s1(0)
     product(1)
     s2(0)
     s3(0)
     s1(1)
+    product(2)
     s4(0)
     s5(0)
     s2(1)
     s3(1)
     s6(0)
     s7(0)
+    s1(2)
     s4(1)
     s5(1)
+    s2(2)
+    s3(2)
     s8(0)
     s6(1)
     s7(1)
+    s4(2)
+    s5(2)
     s8(1)
-    s9(0)
-    s9(1)
+    s6(2)
+    s7(2)
+    s8(2)
+    for i in (0, 1, 2):
+        s9(i)
+    for copy in kept:
+        copy.wait()
     for copy in started:
         copy.wait_send()
 
@@ -347,33 +365,37 @@
     def pair_of(*shape):
         return [pltpu.VMEM(shape, BF16)] * 2
 
+    thin_rows = rows // 3
     sems = [(2, 4, 2)] * 2 + [(2, 4)] * 2 + [(6,)] * 2 + [(2,)] * 8
-    sems += [(2, 2)] * 2 + [(2, 2, 2)] * 2 + [(2,)] * 2 + [(2, 4)] * 2 + [(2, 2)] * 2 + [(2, 2, 2)] * 2 + [(2, 7)] * 4
+    sems += [(3, 2)] * 2 + [(3, 2, 2)] * 2 + [(3,)] * 2 + [(3, 4)] * 2 + [(3, 2)] * 2 + [(3, 2, 2)] * 2 + [(3, 7)] * 4
+    sems += [(2, 2), (3,)]
+    hbm = pl.BlockSpec(memory_space=pl.ANY)
     return pl.pallas_call(
         gamma_kernel,
-        out_shape=jax.ShapeDtypeStruct((2, nz, slots // nz, group), BF16),
-        in_specs=[vmem, smem, vmem, smem, smem],
-        out_specs=vmem,
+        out_shape=jax.ShapeDtypeStruct((2, slots // nz, nz * group), BF16),
+        in_specs=[hbm, smem, vmem, smem, smem],
+        out_specs=hbm,
         scratch_shapes=pair_of(2, 8, rows, width)
         + wide
         + thin
         + [
             pltpu.VMEM((2, group, 2 * group), BF16),
-            pltpu.VMEM((2, nyx, rows, width), F32),
+            pltpu.VMEM((3, 2, nyx, thin_rows, width), F32),
             pltpu.VMEM((group, 128), F32),
         ]
-        + pair_of(2, 2, rows, cols)
-        + pair_of(2, 2, 2, rows, cols)
-        + pair_of(2, rows, cols)
-        + pair_of(2, 4, rows, cols)
-        + pair_of(2, 2, rows, cols // 2)
-        + pair_of(2, 2, 2, rows, cols // 2)
+        + pair_of(3, 2, 2, thin_rows, cols)
+        + pair_of(3, 2, 2, 2, thin_rows, cols)
+        + pair_of(3, 2, thin_rows, cols)
+        + pair_of(3, 4, 2, thin_rows, cols)
+        + pair_of(3, 2, 2, thin_rows, cols // 2)
+        + pair_of(3, 2, 2, 2, thin_rows, cols // 2)
         + [
-            pltpu.VMEM((nyx, width, slots), BF16),
-            pltpu.VMEM((2, rows, width), BF16),
-            pltpu.VMEM((2, 7, rows, slots), BF16),
-            pltpu.VMEM((2, nyx, rows, slots), BF16),
-            pltpu.VMEM((2, slots, group), BF16),
+            pltpu.VMEM((2 * thin_rows, width), F32),
+            pltpu.VMEM((width + slots // nz, 128), F32),
+            pltpu.VMEM((1, slots, 128), F32),
+            pltpu.VMEM((3, 7, 2, thin_rows, slots), BF16),
+            pltpu.VMEM((3, nyx, 2, thin_rows, slots), BF16),
+            pltpu.VMEM((3, 2, slots, 8 * thin_rows), BF16),
         ]
         + [dma(s) for s in sems],
         compiler_params=pltpu.CompilerParams(
@@ -396,7 +418,7 @@
     dest_start = jnp.sum(jnp.where(match, starts[None, :], 0), axis=1)
     dest_length = jnp.sum(jnp.where(match, lengths[None, :], 0), axis=1)
     got = owned_columns(factors, occ_energy, vir_energy, dest_start, dest_length)
-    return jnp.transpose(got, (2, 0, 1, 3)).reshape(got.shape[2], occupied, owners * rows)
+    return jnp.transpose(got, (1, 0, 2))
 
 
 def solution(mesh):

time: 111 us -> 107 us (0.964)
  Pallas kernels: 106 us -> 102 us
    pallas_call x1, Pallas kernels: 106 us -> 102 us  [owned_columns(): pl.pallas_call(gamma_kernel, out_shape=jax.ShapeDtypeStruct((2, slots //...]
    transpose x0 -> x1, local copies, waits for them, and re-layouts: none -> 2.82 us  [per_device(): return jnp.transpose(got, (1, 0, 2))]
    reshape x2 -> x0, local copies, waits for them, and re-layouts: 2.65 us -> none  [per_device(): jnp.transpose(got, (2, 0, 1, 3))]
where the time goes in v5:
time: 107 us
  Pallas kernels  102 us (95%)
  local copies, waits for them, and re-layouts  4.23 us (4%)
    pallas_call x1, Pallas kernels, owned_columns(): pl.pallas_call(gamma_kernel, out_shape=jax.ShapeDtypeStruct((2, slots //...  102 us
    transpose x1, local copies, waits for them, and re-layouts, per_device(): return jnp.transpose(got, (1, 0, 2))  2.82 us

profile of v5, /device:TPU:1, one launch (start us, length us, event | category | flops | bytes accessed | tf_op | source)
XLA Modules:
  0.0 106.6 jit_solution(74682803637893144)
XLA Ops:
  0.0 0.0 copy-start
  0.0 0.7 dynamic-slice_bitcast_fusion
  0.7 0.1 select_reduce_fusion.2
  0.8 0.7 select_reduce_fusion
  1.5 0.0 copy-done
  1.5 0.7 reshape.4.vir_ref
  2.2 101.5 %owned_columns.1 = bf16[2,64,3072]{2,1,0:T(8,128)(2,1)} custom-call(bf16[2,48,1536]{2,1,0:T(8,128)(2,1)} %f_ref.1, f32[2]{0:T(128)} %occ_ref.1, f32[64,48]{1,0:T(8,128)} %reshape.4.vir_ref, s32[64]{0:T(128)} %get-tuple-element.6.start_ref, s32[64]{0:T(128)} %get-tuple-element.5.length_ref), custom_call_target="tpu_custom_call" | custom-call | tf_op jit(solution)/shard_map/owned_columns/pallas_call | solution.py:373
  103.8 2.8 %copy.8 = bf16[64,2,3072]{2,1,0:T(2,128)(2,1)} copy(bf16[64,2,3072]{2,0,1:T(8,128)(2,1)} %bitcast.5) | data formatting | bytes 1572864 | tf_op jit(solution)/shard_map/transpose | solution.py:421
Async XLA Ops:
  0.0 1.5 %copy-start = (f32[3072]{0:T(1024)S(1)}, f32[3072]{0:T(1024)}, u32[]{:S(2)}) copy-start(f32[3072]{0:T(1024)} %param.7) | copy-start | bytes 36868

commit v6 on v5

--- a/solution.py
+++ b/solution.py
@@ -69,14 +69,19 @@
     y_to = ({"y": ring("y", 1)}, {"y": ring("y", -1)})
     x_to = {"xl": flip("xl")}
 
+    order = (0, -1, 1, -2, 2, -3, 3, 4)
+
+    def tile(i, dz):
+        at = order.index(4 if dz == -4 else dz)
+        return cbuf.at[at // 4, i, at % 4]
+
     def z_send(d, step, i):
-        origin = ring("z", (1 - step) if d == 0 else (step - 1))
-        src = f_ref.at[i] if step == 1 else cbuf.at[i, origin]
-        send(src, cbuf.at[i, origin], zs.at[d, step - 1, i], zr.at[d, step - 1, i], z_to[d])
+        sign = -1 if d == 0 else 1
+        src = f_ref.at[i] if step == 1 else tile(i, sign * (step - 1))
+        send(src, tile(i, sign * step), zs.at[d, step - 1, i], zr.at[d, step - 1, i], z_to[d])
 
     def z_arrive(d, step, i):
-        origin = ring("z", -step if d == 0 else step)
-        arrive(cbuf.at[i, origin], zr.at[d, step - 1, i])
+        arrive(tile(i, -step if d == 0 else step), zr.at[d, step - 1, i])
 
     def y_send(d, k, i, dy, other):
         src = f_ref.at[i] if (dy == 0 and not other) else rbuf.at[i, yx(dy, other)]
@@ -94,101 +99,121 @@
 
     for i in (0, 1):
         for d in (0, 1):
-            z_send(d, 1, i)
+            z_send(d, 1, i if d == 0 else 1 - i)
             y_send(d, i, i, 0, False)
         x_send(i, i, 0)
     local = []
     for i in (0, 1):
-        local.append(pltpu.make_async_copy(f_ref.at[i], cbuf.at[i, z], fs.at[0, i]))
+        local.append(pltpu.make_async_copy(f_ref.at[i], tile(i, 0), fs.at[0, i]))
         local.append(pltpu.make_async_copy(f_ref.at[i], rbuf.at[i, yx(0, False)], fs.at[1, i]))
     for copy in local:
         copy.start()
     near_e = jnp.concatenate([vir_ref[pl.ds(z * 8 + k, 1), :] for k in range(8)], axis=1)
     row_e_buf[...] = jnp.broadcast_to(near_e, (128, 8 * rows)).T
-    col_e = jnp.concatenate([vir_ref[pl.ds(k * 8 + yx(0, False), 1), :] for k in range(8)], axis=1)
-    for d in (0, 1):
-        z_arrive(d, 1, 0)
-        z_send(d, 2, 0)
+    far_e = [vir_ref[pl.ds(ring("z", dz) * 8 + yx(0, False), 1), :] for dz in order]
+    col_e = [jnp.concatenate(far_e[4 * g : 4 * g + 4] * 2, axis=1) for g in (0, 1)]
+    for d in (0, 1):
+        z_arrive(d, 1, d)
+        z_send(d, 2, d)
     y_arrive(0, 0, 0, -1, False)
     x_send(2, 0, -1)
     y_send(0, 2, 0, -1, False)
     y_arrive(1, 0, 0, 1, False)
     for d in (0, 1):
-        z_arrive(d, 1, 1)
-        z_send(d, 2, 1)
+        z_arrive(d, 1, 1 - d)
+        z_send(d, 2, 1 - d)
     y_arrive(1, 1, 1, 1, False)
     x_send(3, 1, 1)
     y_send(1, 2, 1, 1, False)
     x_send(4, 0, 1)
     y_arrive(0, 1, 1, -1, False)
-    x_send(5, 1, -1)
-    for d in (0, 1):
-        z_arrive(d, 2, 0)
-        z_send(d, 3, 0)
     x_arrive(0, 0, 0)
     x_arrive(1, 1, 0)
+    y_send(0, 4, 1, 0, True)
+    for d in (0, 1):
+        z_arrive(d, 2, d)
+        z_send(d, 3, d)
     x_arrive(2, 0, -1)
     y_send(0, 3, 0, -1, True)
     for d in (0, 1):
-        z_arrive(d, 2, 1)
-        z_send(d, 3, 1)
+        z_arrive(d, 2, 1 - d)
+        z_send(d, 3, 1 - d)
     x_arrive(3, 1, 1)
     y_send(1, 3, 1, 1, True)
-    z_arrive(0, 3, 0)
-    z_send(0, 4, 0)
-    z_arrive(1, 3, 1)
-    z_send(1, 4, 1)
-    z_arrive(1, 3, 0)
-    z_arrive(0, 3, 1)
+    for d in (0, 1):
+        z_arrive(d, 3, d)
+        z_send(d, 4, d)
     y_arrive(0, 2, 0, -2, False)
     y_arrive(1, 2, 1, 2, False)
+    y_arrive(0, 4, 1, -1, True)
     x_arrive(4, 0, 1)
-    x_arrive(5, 1, -1)
     y_arrive(0, 3, 0, -2, True)
     y_arrive(1, 3, 1, 2, True)
-    z_arrive(0, 4, 0)
-    z_arrive(1, 4, 1)
-
     for copy in local:
         copy.wait()
 
     half = 4 * rows
     side = 8 * rows
-    columns = cbuf[...].reshape(2 * side, width)
-
-    def pair_rows(i, h):
+    mine = pl.ds(pl.multiple_of(core * half, 16), half)
+    theirs = pl.ds(pl.multiple_of((1 - core) * half, 16), half)
+    row_e = row_e_buf[mine, 0:1]
+    lane = lax.broadcasted_iota(jnp.int32, (1, side), 1)
+    low = lane < half
+    occ_j = jnp.where(low, occ_ref[0], occ_ref[1])
+
+    def pair_rows(g, i, h):
         lhs = rbuf[i, pl.ds(h * 4, 4)].reshape(half, width)
-        return lax.dot_general(lhs, columns, (((1,), (1,)), ((), ())), preferred_element_type=F32)
-
-    for i in (0, 1):
-        m_send[i] = pair_rows(i, 1 - core)
-        send(m_send.at[i], m_recv.at[i], ms.at[i], mr.at[i], core_to)
-    for i in (0, 1):
-        m_own[i] = pair_rows(i, core)
-    for i in (0, 1):
-        arrive(m_recv.at[i], mr.at[i])
-        total = m_own[i] + m_recv[i]
-        m_own[i] = total
-        h_send[i] = total.astype(BF16)
-        send(h_send.at[i], hop.at[i], hs.at[i], hr.at[i], (pair_to, cross_to)[i])
-    for i in (0, 1):
-        arrive(hop.at[i], hr.at[i])
-        send(hop.at[i], h_recv.at[i], rs.at[i], rr.at[i], (cross_to, pair_to)[i])
-    for i in (0, 1):
-        arrive(h_recv.at[i], rr.at[i])
-        m_own[i] = m_own[i] + h_recv[i].astype(F32)
-    row_e = row_e_buf[pl.ds(pl.multiple_of(core * half, 16), half), 0:1]
-    mine = pl.ds(pl.multiple_of(core * half, 16), half)
-    for i in (0, 1):
-        for j in (0, 1):
-            denominator = (occ_ref[i] + occ_ref[j]) - row_e - col_e
-            direct = m_own[i, :, pl.ds(j * side, side)]
-            swapped = m_own[j, :, pl.ds(i * side, side)]
-            abuf[i, mine, pl.ds(j * side, side)] = ((2.0 * direct - swapped) / denominator).astype(BF16)
-        send(abuf.at[i, mine], abuf.at[i, mine], as_.at[i], ar.at[i], core_to)
-    theirs = pl.ds(pl.multiple_of((1 - core) * half, 16), half)
-    for i in (0, 1):
-        arrive(abuf.at[i, theirs], ar.at[i])
+        rhs = cbuf[g].reshape(side, width)
+        return lax.dot_general(lhs, rhs, (((1,), (1,)), ((), ())), preferred_element_type=F32)
+
+    def f1(g):
+        for i in (0, 1):
+            m_send[g, i] = pair_rows(g, i, 1 - core)
+            send(m_send.at[g, i], m_recv.at[g, i], ms.at[g, i], mr.at[g, i], core_to)
+        for i in (0, 1):
+            m_own[g, i] = pair_rows(g, i, core)
+
+    def f2(g):
+        for i in (0, 1):
+            arrive(m_recv.at[g, i], mr.at[g, i])
+            total = m_own[g, i] + m_recv[g, i]
+            m_own[g, i] = total
+            h_send[g, i] = total.astype(BF16)
+            send(h_send.at[g, i], hop.at[g, i], hs.at[g, i], hr.at[g, i], (pair_to, cross_to)[i])
+
+    def f3(g):
+        for i in (0, 1):
+            arrive(hop.at[g, i], hr.at[g, i])
+            send(hop.at[g, i], h_recv.at[g, i], rs.at[g, i], rr.at[g, i], (cross_to, pair_to)[i])
+
+    def f4(g):
+        for i in (0, 1):
+            arrive(h_recv.at[g, i], rr.at[g, i])
+            m_own[g, i] = m_own[g, i] + h_recv[g, i].astype(F32)
+        for i in (0, 1):
+            direct = m_own[g, i]
+            turned_over = pltpu.roll(m_own[g, 1 - i], half, 1)
+            swapped = jnp.where(low, direct, turned_over) if i == 0 else jnp.where(low, turned_over, direct)
+            denominator = (occ_ref[i] + occ_j) - row_e - col_e[g]
+            at = pl.ds(g * side, side)
+            abuf[i, mine, at] = ((2.0 * direct - swapped) / denominator).astype(BF16)
+            send(abuf.at[i, mine, at], abuf.at[i, mine, at], as_.at[g, i], ar.at[g, i], core_to)
+
+    f1(0)
+    f2(0)
+    for d in (0, 1):
+        z_arrive(d, 3, 1 - d)
+    f3(0)
+    for d in (0, 1):
+        z_arrive(d, 4, d)
+    f1(1)
+    f2(1)
+    f4(0)
+    f3(1)
+    f4(1)
+    for g in (0, 1):
+        for i in (0, 1):
+            arrive(abuf.at[i, theirs, pl.ds(g * side, side)], ar.at[g, i])
 
     cols = width // 2
     quad = cols // 2
@@ -359,14 +384,14 @@
     dma = pltpu.SemaphoreType.DMA
     vmem = pl.BlockSpec(memory_space=pltpu.VMEM)
     smem = pl.BlockSpec(memory_space=pltpu.SMEM)
-    wide = [pltpu.VMEM((2, half, 2 * group), F32)] * 3
-    thin = [pltpu.VMEM((2, half, 2 * group), BF16)] * 3
+    wide = [pltpu.VMEM((2, 2, half, group), F32)] * 3
+    thin = [pltpu.VMEM((2, 2, half, group), BF16)] * 3
 
     def pair_of(*shape):
         return [pltpu.VMEM(shape, BF16)] * 2
 
     thin_rows = rows // 3
-    sems = [(2, 4, 2)] * 2 + [(2, 4)] * 2 + [(6,)] * 2 + [(2,)] * 8
+    sems = [(2, 4, 2)] * 2 + [(2, 5)] * 2 + [(5,)] * 2 + [(2, 2)] * 8
     sems += [(3, 2)] * 2 + [(3, 2, 2)] * 2 + [(3,)] * 2 + [(3, 4)] * 2 + [(3, 2)] * 2 + [(3, 2, 2)] * 2 + [(3, 7)] * 4
     sems += [(2, 2), (3,)]
     hbm = pl.BlockSpec(memory_space=pl.ANY)
@@ -375,7 +400,7 @@
         out_shape=jax.ShapeDtypeStruct((2, slots // nz, nz * group), BF16),
         in_specs=[hbm, smem, vmem, smem, smem],
         out_specs=hbm,
-        scratch_shapes=pair_of(2, 8, rows, width)
+        scratch_shapes=[pltpu.VMEM((2, 8, rows, width), BF16), pltpu.VMEM((2, 2, 4, rows, width), BF16)]
         + wide
         + thin
         + [

time: 107 us -> 104 us (0.972)
  Pallas kernels: 102 us -> 98.7 us
    pallas_call x1, Pallas kernels: 102 us -> 98.7 us  [owned_columns(): pl.pallas_call(gamma_kernel, out_shape=jax.ShapeDtypeStruct((2, slots //...]
where the time goes in v6:
time: 104 us
  Pallas kernels  98.7 us (95%)
  local copies, waits for them, and re-layouts  4.23 us (4%)
    pallas_call x1, Pallas kernels, owned_columns(): pl.pallas_call(gamma_kernel, out_shape=jax.ShapeDtypeStruct((2, slots //...  98.7 us
    transpose x1, local copies, waits for them, and re-layouts, per_device(): return jnp.transpose(got, (1, 0, 2))  2.82 us

profile of v6, /device:TPU:1, one launch (start us, length us, event | category | flops | bytes accessed | tf_op | source)
XLA Modules:
  0.0 103.8 jit_solution(1847689634523923726)
XLA Ops:
  0.0 0.0 copy-start
  0.0 0.7 dynamic-slice_bitcast_fusion
  0.7 0.1 select_reduce_fusion.2
  0.8 0.7 select_reduce_fusion
  1.5 0.0 copy-done
  1.5 0.7 reshape.4.vir_ref
  2.2 98.7 %owned_columns.1 = bf16[2,64,3072]{2,1,0:T(8,128)(2,1)} custom-call(bf16[2,48,1536]{2,1,0:T(8,128)(2,1)} %f_ref.1, f32[2]{0:T(128)} %occ_ref.1, f32[64,48]{1,0:T(8,128)} %reshape.4.vir_ref, s32[64]{0:T(128)} %get-tuple-element.6.start_ref, s32[64]{0:T(128)} %get-tuple-element.5.length_ref), custom_call_target="tpu_custom_call" | custom-call | tf_op jit(solution)/shard_map/owned_columns/pallas_call | solution.py:398
  100.9 2.8 %copy.8 = bf16[64,2,3072]{2,1,0:T(2,128)(2,1)} copy(bf16[64,2,3072]{2,0,1:T(8,128)(2,1)} %bitcast.5) | data formatting | bytes 1572864 | tf_op jit(solution)/shard_map/transpose | solution.py:446
Async XLA Ops:
  0.0 1.5 %copy-start = (f32[3072]{0:T(1024)S(1)}, f32[3072]{0:T(1024)}, u32[]{:S(2)}) copy-start(f32[3072]{0:T(1024)} %param.7) | copy-start | bytes 36868

commit v7 on v6

--- a/solution.py
+++ b/solution.py
@@ -22,10 +22,10 @@
 
 def gamma_kernel(
     f_ref, occ_ref, vir_ref, start_ref, length_ref, out_ref,
-    rbuf, cbuf, m_send, m_own, m_recv, h_send, h_recv, hop, abuf, part, row_e_buf,
+    rbuf, cbuf, m_send, m_own, m_recv, h_send, h_recv, abuf, part, row_e_buf,
     ya_out, ya_in, yb_out, yb_in, yc_out, yc_in, xa_out, xa_in, xb_out, xb_in, xc_out, xc_in,
     gamma, window, spread, pick_out, pick_in, turned,
-    zs, zr, ys, yr, xs, xr, ms, mr, hs, hr, rs, rr, as_, ar,
+    zs, zr, ys, yr, xs, xr, ms, mr, hs, hr, as_, ar,
     yas, yar, ybs, ybr, ycs, ycr, xas, xar, xbs, xbr, xcs, xcr, qs, qr, ts, tr, fs, os_,
 ):
     z, y, xl, xh, core = (lax.axis_index(n) for n in ("z", "y", "xl", "xh", "core"))
@@ -39,8 +39,8 @@
     z_peers = [{"z": ring("z", dz)} for dz in z_steps]
     core_to = {"core": flip("core")}
     pair_to = {"xl": flip("xl")}
-    cross_to = {"xh": flip("xh"), "xl": flip("xl")}
-    peers = [z_peers[-2], z_peers[-1], yx_peers[4], yx_peers[5], pair_to, cross_to, core_to]
+    xh_to = {"xh": flip("xh")}
+    peers = [z_peers[-2], z_peers[-1], yx_peers[4], yx_peers[5], pair_to, xh_to, core_to]
     for peer in peers:
         pl.semaphore_signal(barrier, inc=1, device_id=peer, device_id_type=pl.DeviceIdType.MESH)
     pl.semaphore_wait(barrier, len(peers))
@@ -65,6 +65,9 @@
     def yx(dy, other):
         return ring("y", dy) * 2 + (flip("xl") if other else xl)
 
+    def own_tile(i, at):
+        return rbuf.at[i, pl.ds(pl.multiple_of(at * rows, 16), rows)]
+
     z_to = ({"z": ring("z", 1)}, {"z": ring("z", -1)})
     y_to = ({"y": ring("y", 1)}, {"y": ring("y", -1)})
     x_to = {"xl": flip("xl")}
@@ -84,18 +87,18 @@
         arrive(tile(i, -step if d == 0 else step), zr.at[d, step - 1, i])
 
     def y_send(d, k, i, dy, other):
-        src = f_ref.at[i] if (dy == 0 and not other) else rbuf.at[i, yx(dy, other)]
-        send(src, rbuf.at[i, yx(dy, other)], ys.at[d, k], yr.at[d, k], y_to[d])
+        src = f_ref.at[i] if (dy == 0 and not other) else own_tile(i, yx(dy, other))
+        send(src, own_tile(i, yx(dy, other)), ys.at[d, k], yr.at[d, k], y_to[d])
 
     def y_arrive(d, k, i, dy, other):
-        arrive(rbuf.at[i, yx(dy, other)], yr.at[d, k])
+        arrive(own_tile(i, yx(dy, other)), yr.at[d, k])
 
     def x_send(k, i, dy):
-        src = f_ref.at[i] if dy == 0 else rbuf.at[i, yx(dy, False)]
-        send(src, rbuf.at[i, yx(dy, False)], xs.at[k], xr.at[k], x_to)
+        src = f_ref.at[i] if dy == 0 else own_tile(i, yx(dy, False))
+        send(src, own_tile(i, yx(dy, False)), xs.at[k], xr.at[k], x_to)
 
     def x_arrive(k, i, dy):
-        arrive(rbuf.at[i, yx(dy, True)], xr.at[k])
+        arrive(own_tile(i, yx(dy, True)), xr.at[k])
 
     for i in (0, 1):
         for d in (0, 1):
@@ -105,7 +108,7 @@
     local = []
     for i in (0, 1):
         local.append(pltpu.make_async_copy(f_ref.at[i], tile(i, 0), fs.at[0, i]))
-        local.append(pltpu.make_async_copy(f_ref.at[i], rbuf.at[i, yx(0, False)], fs.at[1, i]))
+        local.append(pltpu.make_async_copy(f_ref.at[i], own_tile(i, yx(0, False)), fs.at[1, i]))
     for copy in local:
         copy.start()
     near_e = jnp.concatenate([vir_ref[pl.ds(z * 8 + k, 1), :] for k in range(8)], axis=1)
@@ -152,68 +155,75 @@
     for copy in local:
         copy.wait()
 
-    half = 4 * rows
     side = 8 * rows
-    mine = pl.ds(pl.multiple_of(core * half, 16), half)
-    theirs = pl.ds(pl.multiple_of((1 - core) * half, 16), half)
-    row_e = row_e_buf[mine, 0:1]
+    half = side // 2
+    thin = rows // 3
+    band = 8 * thin
+    share = band // 2
     lane = lax.broadcasted_iota(jnp.int32, (1, side), 1)
     low = lane < half
     occ_j = jnp.where(low, occ_ref[0], occ_ref[1])
 
-    def pair_rows(g, i, h):
-        lhs = rbuf[i, pl.ds(h * 4, 4)].reshape(half, width)
+    def rows_of(c, h):
+        return pl.ds(pl.multiple_of(c * band + h * share, 16), share)
+
+    def pair_rows(g, c, h):
+        lhs = rbuf[:, rows_of(c, h)].reshape(2 * share, width)
         rhs = cbuf[g].reshape(side, width)
-        return lax.dot_general(lhs, rhs, (((1,), (1,)), ((), ())), preferred_element_type=F32)
-
-    def f1(g):
+        res = lax.dot_general(lhs, rhs, (((1,), (1,)), ((), ())), preferred_element_type=F32)
+        return res.reshape(2, share, side)
+
+    def f1(g, c):
+        m_send[g, c] = pair_rows(g, c, 1 - core)
+        send(m_send.at[g, c], m_recv.at[g, c], ms.at[g, c], mr.at[g, c], core_to)
+        m_own[g, c] = pair_rows(g, c, core)
+
+    def f2(g, c):
+        arrive(m_recv.at[g, c], mr.at[g, c])
+        total = m_own[g, c] + m_recv[g, c]
+        m_own[g, c] = total
+        h_send[g, c] = total.astype(BF16)
+        send(h_send.at[g, c], h_recv.at[g, c], hs.at[g, c], hr.at[g, c], xh_to)
+
+    def f4(g, c):
+        arrive(h_recv.at[g, c], hr.at[g, c])
+        m_own[g, c] = m_own[g, c] + h_recv[g, c].astype(F32)
+        row_e = row_e_buf[rows_of(c, core), 0:1]
+        at = pl.ds(g * side, side)
         for i in (0, 1):
-            m_send[g, i] = pair_rows(g, i, 1 - core)
-            send(m_send.at[g, i], m_recv.at[g, i], ms.at[g, i], mr.at[g, i], core_to)
-        for i in (0, 1):
-            m_own[g, i] = pair_rows(g, i, core)
-
-    def f2(g):
-        for i in (0, 1):
-            arrive(m_recv.at[g, i], mr.at[g, i])
-            total = m_own[g, i] + m_recv[g, i]
-            m_own[g, i] = total
-            h_send[g, i] = total.astype(BF16)
-            send(h_send.at[g, i], hop.at[g, i], hs.at[g, i], hr.at[g, i], (pair_to, cross_to)[i])
-
-    def f3(g):
-        for i in (0, 1):
-            arrive(hop.at[g, i], hr.at[g, i])
-            send(hop.at[g, i], h_recv.at[g, i], rs.at[g, i], rr.at[g, i], (cross_to, pair_to)[i])
-
-    def f4(g):
-        for i in (0, 1):
-            arrive(h_recv.at[g, i], rr.at[g, i])
-            m_own[g, i] = m_own[g, i] + h_recv[g, i].astype(F32)
-        for i in (0, 1):
-            direct = m_own[g, i]
-            turned_over = pltpu.roll(m_own[g, 1 - i], half, 1)
+            direct = m_own[g, c, i]
+            turned_over = pltpu.roll(m_own[g, c, 1 - i], half, 1)
             swapped = jnp.where(low, direct, turned_over) if i == 0 else jnp.where(low, turned_over, direct)
             denominator = (occ_ref[i] + occ_j) - row_e - col_e[g]
-            at = pl.ds(g * side, side)
-            abuf[i, mine, at] = ((2.0 * direct - swapped) / denominator).astype(BF16)
-            send(abuf.at[i, mine, at], abuf.at[i, mine, at], as_.at[g, i], ar.at[g, i], core_to)
-
-    f1(0)
-    f2(0)
+            abuf[i, rows_of(c, core), at] = ((2.0 * direct - swapped) / denominator).astype(BF16)
+        mine = abuf.at[:, rows_of(c, core), at]
+        send(mine, mine, as_.at[g, c], ar.at[g, c], core_to)
+
+    def f5(c):
+        for g in (0, 1):
+            arrive(abuf.at[:, rows_of(c, 1 - core), pl.ds(g * side, side)], ar.at[g, c])
+
+    f1(0, 0)
+    f1(0, 1)
+    f2(0, 0)
+    f1(0, 2)
+    f2(0, 1)
+    f2(0, 2)
     for d in (0, 1):
         z_arrive(d, 3, 1 - d)
-    f3(0)
     for d in (0, 1):
         z_arrive(d, 4, d)
-    f1(1)
-    f2(1)
-    f4(0)
-    f3(1)
-    f4(1)
-    for g in (0, 1):
-        for i in (0, 1):
-            arrive(abuf.at[i, theirs, pl.ds(g * side, side)], ar.at[g, i])
+    f1(1, 0)
+    f1(1, 1)
+    f2(1, 0)
+    f4(0, 0)
+    f1(1, 2)
+    f2(1, 1)
+    f2(1, 2)
+    f4(0, 1)
+    f4(1, 0)
+    f4(0, 2)
+    f5(0)
 
     cols = width // 2
     quad = cols // 2
@@ -226,8 +236,6 @@
 
     slots = spread.shape[1]
     capacity = slots // 8
-    thin = rows // 3
-    band = 8 * thin
     window[pl.ds(width, capacity), :] = jnp.zeros((capacity, 128), F32)
 
     def product(c):
@@ -341,10 +349,14 @@
     kept = []
     product(0)
     s1(0)
+    f4(1, 1)
+    f5(1)
     product(1)
     s2(0)
     s3(0)
     s1(1)
+    f4(1, 2)
+    f5(2)
     product(2)
     s4(0)
     s5(0)
@@ -378,20 +390,19 @@
     occupied, rows, width = factors.shape
     nz, nyx = lax.axis_size("z"), lax.axis_size(ROW)
     group = rows * nyx
-    half = group // 2
     slots = 8 * width // (3 * nyx)
     cols = width // 2
     dma = pltpu.SemaphoreType.DMA
     vmem = pl.BlockSpec(memory_space=pltpu.VMEM)
     smem = pl.BlockSpec(memory_space=pltpu.SMEM)
-    wide = [pltpu.VMEM((2, 2, half, group), F32)] * 3
-    thin = [pltpu.VMEM((2, 2, half, group), BF16)] * 3
+    wide = [pltpu.VMEM((2, 3, 2, group // 6, group), F32)] * 3
+    thin = [pltpu.VMEM((2, 3, 2, group // 6, group), BF16)] * 2
 
     def pair_of(*shape):
         return [pltpu.VMEM(shape, BF16)] * 2
 
     thin_rows = rows // 3
-    sems = [(2, 4, 2)] * 2 + [(2, 5)] * 2 + [(5,)] * 2 + [(2, 2)] * 8
+    sems = [(2, 4, 2)] * 2 + [(2, 5)] * 2 + [(5,)] * 2 + [(2, 3)] * 6
     sems += [(3, 2)] * 2 + [(3, 2, 2)] * 2 + [(3,)] * 2 + [(3, 4)] * 2 + [(3, 2)] * 2 + [(3, 2, 2)] * 2 + [(3, 7)] * 4
     sems += [(2, 2), (3,)]
     hbm = pl.BlockSpec(memory_space=pl.ANY)
@@ -400,7 +411,7 @@
         out_shape=jax.ShapeDtypeStruct((2, slots // nz, nz * group), BF16),
         in_specs=[hbm, smem, vmem, smem, smem],
         out_specs=hbm,
-        scratch_shapes=[pltpu.VMEM((2, 8, rows, width), BF16), pltpu.VMEM((2, 2, 4, rows, width), BF16)]
+        scratch_shapes=[pltpu.VMEM((2, group, width), BF16), pltpu.VMEM((2, 2, 4, rows, width), BF16)]
         + wide
         + thin
         + [

time: 104 us -> 96 us (0.923)
  Pallas kernels: 98.7 us -> 90.7 us
    pallas_call x1, Pallas kernels: 98.7 us -> 90.7 us  [owned_columns(): pl.pallas_call(gamma_kernel, out_shape=jax.ShapeDtypeStruct((2, slots //...]
where the time goes in v7:
time: 96 us; the launch traced here: 95.8 us
  Pallas kernels  90.7 us (94%)
  local copies, waits for them, and re-layouts  4.23 us (4%)
    pallas_call x1, Pallas kernels, owned_columns(): pl.pallas_call(gamma_kernel, out_shape=jax.ShapeDtypeStruct((2, slots //...  90.7 us
    transpose x1, local copies, waits for them, and re-layouts, per_device(): return jnp.transpose(got, (1, 0, 2))  2.82 us

profile of v7, /device:TPU:1, one launch (start us, length us, event | category | flops | bytes accessed | tf_op | source)
XLA Modules:
  0.0 95.8 jit_solution(2535736583488500880)
XLA Ops:
  0.0 0.0 copy-start
  0.0 0.7 dynamic-slice_bitcast_fusion
  0.7 0.1 select_reduce_fusion.2
  0.8 0.7 select_reduce_fusion
  1.5 0.0 copy-done
  1.5 0.7 reshape.4.vir_ref
  2.2 90.7 %owned_columns.1 = bf16[2,64,3072]{2,1,0:T(8,128)(2,1)} custom-call(bf16[2,48,1536]{2,1,0:T(8,128)(2,1)} %f_ref.1, f32[2]{0:T(128)} %occ_ref.1, f32[64,48]{1,0:T(8,128)} %reshape.4.vir_ref, s32[64]{0:T(128)} %get-tuple-element.6.start_ref, s32[64]{0:T(128)} %get-tuple-element.5.length_ref), custom_call_target="tpu_custom_call" | custom-call | tf_op jit(solution)/shard_map/owned_columns/pallas_call | solution.py:409
  92.9 2.8 %copy.8 = bf16[64,2,3072]{2,1,0:T(2,128)(2,1)} copy(bf16[64,2,3072]{2,0,1:T(8,128)(2,1)} %bitcast.5) | data formatting | bytes 1572864 | tf_op jit(solution)/shard_map/transpose | solution.py:457
Async XLA Ops:
  0.0 1.5 %copy-start = (f32[3072]{0:T(1024)S(1)}, f32[3072]{0:T(1024)}, u32[]{:S(2)}) copy-start(f32[3072]{0:T(1024)} %param.7) | copy-start | bytes 36868

commit v8 on v7

--- a/solution.py
+++ b/solution.py
@@ -9,6 +9,7 @@
 VIR = ("xh", "core")
 F32 = jnp.float32
 BF16 = jnp.bfloat16
+LEFT = 640
 
 
 def ring(axis, shift):
@@ -23,10 +24,10 @@
 def gamma_kernel(
     f_ref, occ_ref, vir_ref, start_ref, length_ref, out_ref,
     rbuf, cbuf, m_send, m_own, m_recv, h_send, h_recv, abuf, part, row_e_buf,
-    ya_out, ya_in, yb_out, yb_in, yc_out, yc_in, xa_out, xa_in, xb_out, xb_in, xc_out, xc_in,
+    yb_out, yb_in, yc_out, yc_in, xa_out, xa_in, xc_out, xc_in,
     gamma, window, spread, pick_out, pick_in, turned,
     zs, zr, ys, yr, xs, xr, ms, mr, hs, hr, as_, ar,
-    yas, yar, ybs, ybr, ycs, ycr, xas, xar, xbs, xbr, xcs, xcr, qs, qr, ts, tr, fs, os_,
+    ybs, ybr, ycs, ycr, xas, xar, xcs, xcr, qs, qr, ts, tr, fs, os_,
 ):
     z, y, xl, xh, core = (lax.axis_index(n) for n in ("z", "y", "xl", "xh", "core"))
     rows = f_ref.shape[1]
@@ -111,9 +112,13 @@
         local.append(pltpu.make_async_copy(f_ref.at[i], own_tile(i, yx(0, False)), fs.at[1, i]))
     for copy in local:
         copy.start()
-    near_e = jnp.concatenate([vir_ref[pl.ds(z * 8 + k, 1), :] for k in range(8)], axis=1)
+    def line(at):
+        return jnp.concatenate([vir_ref[pl.ds(3 * at + k, 1), :] for k in range(3)], axis=1)
+
+    near_e = line(z)
     row_e_buf[...] = jnp.broadcast_to(near_e, (128, 8 * rows)).T
-    far_e = [vir_ref[pl.ds(ring("z", dz) * 8 + yx(0, False), 1), :] for dz in order]
+    back = lax.rem((8 - yx(0, False)) * rows, 8 * rows)
+    far_e = [pltpu.roll(line(ring("z", dz)), back, 1)[:, :rows] for dz in order]
     col_e = [jnp.concatenate(far_e[4 * g : 4 * g + 4] * 2, axis=1) for g in (0, 1)]
     for d in (0, 1):
         z_arrive(d, 1, d)
@@ -225,11 +230,12 @@
     f4(0, 2)
     f5(0)
 
-    cols = width // 2
-    quad = cols // 2
+    cols = LEFT
     me = yx(0, False)
     mate = yx(0, True)
-    left, right = pl.ds(0, cols), pl.ds(cols, cols)
+    left, right = pl.ds(0, cols), pl.ds(cols, width - cols)
+    y_steps = (2, 1, -1)
+    y_peers = [{"y": ring("y", dy)} for dy in y_steps]
 
     def wide(ref):
         return ref[...].astype(F32)
@@ -244,68 +250,46 @@
         part[c] = res.reshape(2, 8, thin, width)
 
     def s1(i):
-        for d in (0, 1):
-            ya_out[i, d] = part[i, :, ring("y", 2) * 2 + d, :, left].astype(BF16)
-            send(ya_out.at[i, d], ya_in.at[i, d], yas.at[i, d], yar.at[i, d], y_to[d])
-        for k, dy in enumerate((2, 1, -1, 0)):
+        for k, dy in enumerate(y_steps):
+            there = pl.ds(ring("y", dy) * 2, 2)
+            yb_out[i, k] = part[i, :, there, :, left].astype(BF16)
+            send(yb_out.at[i, k], yb_in.at[i, k], ybs.at[i, k], ybr.at[i, k], y_peers[k])
+        for k, dy in enumerate(y_steps + (0,)):
             xa_out[i, k] = part[i, :, yx(dy, True), :, right].astype(BF16)
             send(xa_out.at[i, k], xa_in.at[i, k], xas.at[i, k], xar.at[i, k], x_to)
-        for d in (0, 1):
-            yb_send(i, d, 1 - d, part[i, :, ring("y", 1 - 2 * d) * 2 + 1 - d, :, left])
-
-    def yb_send(i, d, e, value):
-        yb_out[i, d, e] = value.astype(BF16)
-        send(yb_out.at[i, d, e], yb_in.at[i, d, e], ybs.at[i, d, e], ybr.at[i, d, e], y_to[d])
-
-    def s2(i):
-        for d in (0, 1):
-            arrive(ya_in.at[i, d], yar.at[i, d])
-            yb_send(i, d, d, part[i, :, ring("y", 1 - 2 * d) * 2 + d, :, left] + wide(ya_in.at[i, d]))
-
-    def xc_send(i, d, e, value):
-        xc_out[i, d, e] = value.astype(BF16)
-        send(xc_out.at[i, d, e], xc_in.at[i, d, e], xcs.at[i, d, e], xcr.at[i, d, e], y_to[d])
-
-    def x_sum(i, k, dy, e):
-        at = pl.ds(cols + e * quad, quad)
-        return part[i, :, yx(dy, False), :, at] + xa_in[i, k, :, :, pl.ds(e * quad, quad)].astype(F32)
+
+    def x_sum(i, k, dy):
+        arrive(xa_in.at[i, k], xar.at[i, k])
+        return part[i, :, yx(dy, False), :, right] + wide(xa_in.at[i, k])
 
     def s3(i):
-        arrive(xa_in.at[i, 0], xar.at[i, 0])
-        for d in (0, 1):
-            xb_out[i, d] = x_sum(i, 0, 2, d).astype(BF16)
-            send(xb_out.at[i, d], xb_in.at[i, d], xbs.at[i, d], xbr.at[i, d], y_to[d])
-        for d in (0, 1):
-            arrive(xa_in.at[i, 1 + d], xar.at[i, 1 + d])
-            xc_send(i, d, 1 - d, x_sum(i, 1 + d, 1 - 2 * d, 1 - d))
-
-    def s4(i):
-        for d in (0, 1):
-            arrive(xb_in.at[i, d], xbr.at[i, d])
-            xc_send(i, d, d, x_sum(i, 1 + d, 1 - 2 * d, d) + wide(xb_in.at[i, d]))
+        for k, dy in enumerate(y_steps):
+            xc_out[i, k] = x_sum(i, k, dy).astype(BF16)
+            send(xc_out.at[i, k], xc_in.at[i, k], xcs.at[i, k], xcr.at[i, k], y_peers[k])
+
+    def y_sum(i, e):
+        total = part[i, :, ring("y", 0) * 2 + e, :, left]
+        for k in range(3):
+            total = total + yb_in[i, k, :, e].astype(F32)
+        return total
 
     def s5(i):
-        for d in (0, 1):
-            for e in (1 - d, d):
-                arrive(yb_in.at[i, d, e], ybr.at[i, d, e])
-        far = part[i, :, mate, :, left] + wide(yb_in.at[i, 0, 1 - xl]) + wide(yb_in.at[i, 1, 1 - xl])
-        yc_out[i] = far.astype(BF16)
+        for k in range(3):
+            arrive(yb_in.at[i, k], ybr.at[i, k])
+        yc_out[i] = y_sum(i, 1 - xl).astype(BF16)
         send(yc_out.at[i], yc_in.at[i], ycs.at[i], ycr.at[i], x_to)
 
     def rounded(total):
         return total.astype(BF16).astype(F32).reshape(2 * thin, total.shape[2])
 
     def s6(i):
-        arrive(xa_in.at[i, 3], xar.at[i, 3])
-        for d in (0, 1):
-            for e in (1 - d, d):
-                arrive(xc_in.at[i, d, e], xcr.at[i, d, e])
-        for e in (0, 1):
-            total = x_sum(i, 3, 0, e) + wide(xc_in.at[i, 0, e]) + wide(xc_in.at[i, 1, e])
-            gamma[:, pl.ds(cols + e * quad, quad)] = rounded(total)
-        near = part[i, :, me, :, left] + wide(yb_in.at[i, 0, xl]) + wide(yb_in.at[i, 1, xl])
+        total = x_sum(i, 3, 0)
+        for k in range(3):
+            arrive(xc_in.at[i, k], xcr.at[i, k])
+            total = total + wide(xc_in.at[i, k])
+        gamma[:, right] = rounded(total)
         arrive(yc_in.at[i], ycr.at[i])
-        gamma[:, left] = rounded(near + wide(yc_in.at[i]))
+        gamma[:, left] = rounded(y_sum(i, xl) + wide(yc_in.at[i]))
 
     row_at = lax.broadcasted_iota(jnp.int32, (capacity, 128), 0)
 
@@ -352,27 +336,21 @@
     f4(1, 1)
     f5(1)
     product(1)
-    s2(0)
     s3(0)
     s1(1)
     f4(1, 2)
     f5(2)
     product(2)
-    s4(0)
     s5(0)
-    s2(1)
     s3(1)
+    s1(2)
     s6(0)
     s7(0)
-    s1(2)
-    s4(1)
     s5(1)
-    s2(2)
     s3(2)
     s8(0)
     s6(1)
     s7(1)
-    s4(2)
     s5(2)
     s8(1)
     s6(2)
@@ -391,7 +369,7 @@
     nz, nyx = lax.axis_size("z"), lax.axis_size(ROW)
     group = rows * nyx
     slots = 8 * width // (3 * nyx)
-    cols = width // 2
+    cols = LEFT
     dma = pltpu.SemaphoreType.DMA
     vmem = pl.BlockSpec(memory_space=pltpu.VMEM)
     smem = pl.BlockSpec(memory_space=pltpu.SMEM)
@@ -403,7 +381,7 @@
 
     thin_rows = rows // 3
     sems = [(2, 4, 2)] * 2 + [(2, 5)] * 2 + [(5,)] * 2 + [(2, 3)] * 6
-    sems += [(3, 2)] * 2 + [(3, 2, 2)] * 2 + [(3,)] * 2 + [(3, 4)] * 2 + [(3, 2)] * 2 + [(3, 2, 2)] * 2 + [(3, 7)] * 4
+    sems += [(3, 3)] * 2 + [(3,)] * 2 + [(3, 4)] * 2 + [(3, 3)] * 2 + [(3, 7)] * 4
     sems += [(2, 2), (3,)]
     hbm = pl.BlockSpec(memory_space=pl.ANY)
     return pl.pallas_call(
@@ -419,12 +397,10 @@
             pltpu.VMEM((3, 2, nyx, thin_rows, width), F32),
             pltpu.VMEM((group, 128), F32),
         ]
-        + pair_of(3, 2, 2, thin_rows, cols)
-        + pair_of(3, 2, 2, 2, thin_rows, cols)
+        + pair_of(3, 3, 2, 2, thin_rows, cols)
         + pair_of(3, 2, thin_rows, cols)
-        + pair_of(3, 4, 2, thin_rows, cols)
-        + pair_of(3, 2, 2, thin_rows, cols // 2)
-        + pair_of(3, 2, 2, 2, thin_rows, cols // 2)
+        + pair_of(3, 4, 2, thin_rows, width - cols)
+        + pair_of(3, 3, 2, thin_rows, width - cols)
         + [
             pltpu.VMEM((2 * thin_rows, width), F32),
             pltpu.VMEM((width + slots // nz, 128), F32),
@@ -438,7 +414,7 @@
             collective_id=0, has_side_effects=True, vmem_limit_bytes=60 * 1024 * 1024
         ),
         name="owned_columns",
-    )(factors, occ_energy, vir_energy.reshape(nz * nyx, rows), start, length)
+    )(factors, occ_energy, vir_energy.reshape(nz * group // 128, 128), start, length)
 
 
 def per_device(factors, occ_energy, vir_energy, block_lengths, block_owner):

time: 96 us -> 94.3 us (0.982)
  no operation moved by 1% of the time
where the time goes in v8:
time: 94.3 us; the launch traced here: 94.1 us
  Pallas kernels  89.8 us (95%)
  local copies, waits for them, and re-layouts  3.52 us (4%)
    pallas_call x1, Pallas kernels, owned_columns(): pl.pallas_call(gamma_kernel, out_shape=jax.ShapeDtypeStruct((2, slots //...  89.8 us
    transpose x1, local copies, waits for them, and re-layouts, per_device(): return jnp.transpose(got, (1, 0, 2))  2.82 us

profile of v8, /device:TPU:1, one launch (start us, length us, event | category | flops | bytes accessed | tf_op | source)
XLA Modules:
  0.0 94.1 jit_solution(3908919686758360090)
XLA Ops:
  0.0 0.7 dynamic-slice_bitcast_fusion
  0.7 0.1 select_reduce_fusion.2
  0.8 0.7 select_reduce_fusion
  1.5 89.8 %owned_columns.1 = bf16[2,64,3072]{2,1,0:T(8,128)(2,1)} custom-call(bf16[2,48,1536]{2,1,0:T(8,128)(2,1)} %f_ref.1, f32[2]{0:T(128)} %occ_ref.1, f32[24,128]{1,0:T(8,128)} %bitcast.7, s32[64]{0:T(128)} %get-tuple-element.6.start_ref, s32[64]{0:T(128)} %get-tuple-element.5.length_ref), custom_call_target="tpu_custom_call" | custom-call | tf_op jit(solution)/shard_map/owned_columns/pallas_call | solution.py:387
  91.3 2.8 %copy.7 = bf16[64,2,3072]{2,1,0:T(2,128)(2,1)} copy(bf16[64,2,3072]{2,0,1:T(8,128)(2,1)} %bitcast.6) | data formatting | bytes 1572864 | tf_op jit(solution)/shard_map/transpose | solution.py:433

commit v9 on v8

--- a/solution.py
+++ b/solution.py
@@ -22,17 +22,26 @@
 
 
 def gamma_kernel(
-    f_ref, occ_ref, vir_ref, start_ref, length_ref, out_ref,
+    f_ref, occ_in, vir_in, start_in, length_in, out_ref,
+    occ_ref, vir_ref, start_ref, length_ref,
     rbuf, cbuf, m_send, m_own, m_recv, h_send, h_recv, abuf, part, row_e_buf,
     yb_out, yb_in, yc_out, yc_in, xa_out, xa_in, xc_out, xc_in,
     gamma, window, spread, pick_out, pick_in, turned,
     zs, zr, ys, yr, xs, xr, ms, mr, hs, hr, as_, ar,
-    ybs, ybr, ycs, ycr, xas, xar, xcs, xcr, qs, qr, ts, tr, fs, os_,
+    ybs, ybr, ycs, ycr, xas, xar, xcs, xcr, qs, qr, ts, tr, fs, os_, es,
 ):
     z, y, xl, xh, core = (lax.axis_index(n) for n in ("z", "y", "xl", "xh", "core"))
     rows = f_ref.shape[1]
     width = f_ref.shape[2]
 
+    fetched = [
+        pltpu.make_async_copy(src, dst, es.at[k])
+        for k, (src, dst) in enumerate(
+            [(occ_in, occ_ref), (vir_in, vir_ref), (start_in, start_ref), (length_in, length_ref)]
+        )
+    ]
+    for copy in fetched:
+        copy.start()
     barrier = pltpu.get_barrier_semaphore()
     yx_steps = [(2, True), (2, False), (1, True), (-1, True), (1, False), (-1, False), (0, True)]
     yx_peers = [{"y": ring("y", dy), "xl": flip("xl") if other else xl} for dy, other in yx_steps]
@@ -112,6 +121,9 @@
         local.append(pltpu.make_async_copy(f_ref.at[i], own_tile(i, yx(0, False)), fs.at[1, i]))
     for copy in local:
         copy.start()
+    for copy in fetched:
+        copy.wait()
+
     def line(at):
         return jnp.concatenate([vir_ref[pl.ds(3 * at + k, 1), :] for k in range(3)], axis=1)
 
@@ -371,8 +383,6 @@
     slots = 8 * width // (3 * nyx)
     cols = LEFT
     dma = pltpu.SemaphoreType.DMA
-    vmem = pl.BlockSpec(memory_space=pltpu.VMEM)
-    smem = pl.BlockSpec(memory_space=pltpu.SMEM)
     wide = [pltpu.VMEM((2, 3, 2, group // 6, group), F32)] * 3
     thin = [pltpu.VMEM((2, 3, 2, group // 6, group), BF16)] * 2
 
@@ -382,14 +392,20 @@
     thin_rows = rows // 3
     sems = [(2, 4, 2)] * 2 + [(2, 5)] * 2 + [(5,)] * 2 + [(2, 3)] * 6
     sems += [(3, 3)] * 2 + [(3,)] * 2 + [(3, 4)] * 2 + [(3, 3)] * 2 + [(3, 7)] * 4
-    sems += [(2, 2), (3,)]
+    sems += [(2, 2), (3,), (4,)]
     hbm = pl.BlockSpec(memory_space=pl.ANY)
     return pl.pallas_call(
         gamma_kernel,
         out_shape=jax.ShapeDtypeStruct((2, slots // nz, nz * group), BF16),
-        in_specs=[hbm, smem, vmem, smem, smem],
+        in_specs=[hbm] * 5,
         out_specs=hbm,
-        scratch_shapes=[pltpu.VMEM((2, group, width), BF16), pltpu.VMEM((2, 2, 4, rows, width), BF16)]
+        scratch_shapes=[
+            pltpu.SMEM((2,), F32),
+            pltpu.VMEM((nz * group // 128, 128), F32),
+            pltpu.SMEM((nz * nyx,), jnp.int32),
+            pltpu.SMEM((nz * nyx,), jnp.int32),
+        ]
+        + [pltpu.VMEM((2, group, width), BF16), pltpu.VMEM((2, 2, 4, rows, width), BF16)]
         + wide
         + thin
         + [

time: 94.3 us -> 93.5 us (level)
  no operation moved by 1% of the time
where the time goes in v9:
time: 93.5 us; the launch traced here: 93.3 us
  Pallas kernels  89 us (95%)
  local copies, waits for them, and re-layouts  3.52 us (4%)
    pallas_call x1, Pallas kernels, owned_columns(): pl.pallas_call(gamma_kernel, out_shape=jax.ShapeDtypeStruct((2, slots //...  89 us
    transpose x1, local copies, waits for them, and re-layouts, per_device(): return jnp.transpose(got, (1, 0, 2))  2.82 us

profile of v9, /device:TPU:1, one launch (start us, length us, event | category | flops | bytes accessed | tf_op | source)
XLA Modules:
  0.0 93.3 jit_solution(10874626851561047511)
XLA Ops:
  0.0 0.7 dynamic-slice_bitcast_fusion
  0.7 0.1 select_reduce_fusion.2
  0.8 0.7 select_reduce_fusion
  1.5 89.0 %owned_columns.1 = bf16[2,64,3072]{2,1,0:T(8,128)(2,1)} custom-call(bf16[2,48,1536]{2,1,0:T(8,128)(2,1)} %f_ref.1, f32[2]{0:T(128)} %occ_in.1, f32[24,128]{1,0:T(8,128)} %bitcast.7, s32[64]{0:T(128)} %get-tuple-element.6.start_in, s32[64]{0:T(128)} %get-tuple-element.5.length_in), custom_call_target="tpu_custom_call" | custom-call | tf_op jit(solution)/shard_map/owned_columns/pallas_call | solution.py:397
  90.5 2.8 %copy.7 = bf16[64,2,3072]{2,1,0:T(2,128)(2,1)} copy(bf16[64,2,3072]{2,0,1:T(8,128)(2,1)} %bitcast.6) | data formatting | bytes 1572864 | tf_op jit(solution)/shard_map/transpose | solution.py:449
